TPU v7x, 32 devices: a whole 2x2x4 slice. The times are simulated.
32 devices in a mesh: groups: 2 (over y), tile: 4 (over z), line: 2 (over x), sub: 2 (over core).
Axes of the slice: x: 2, y: 2, z: 4, core: 2. Of those that a mesh axis runs over, the one named last changes fastest.
Arguments:
- traces: bfloat16 [4, 64, 1024, 1024], P(('groups', 'line'), None, 'tile', 'sub'), parts along dimension 0, may hold values from -6 to 6
- mute_index: int32 [1024], replicated, may hold values from 0 to 15
- freq_bins: int32 [4], replicated, may hold values from 0 to 3, each once
Outputs:
- multiples: float32 [2, 4, 2048, 1024], P(None, 'tile', ('groups', 'line'), 'sub'), parts along dimension 2
There are 2 independent parts, one for each index of `groups`. A program takes and returns all parts, laid end to end along the dimension named above; an argument that names none is the same for every part. Nothing has to cross between parts.
Inputs may be any that keep to these rules, and one draw needn't show every extreme that they name: `freq_bins`: every bin number appears in exactly one slot.
All inputs are finite; a program needn't handle non-finite values.
Results may differ from a plain program's by a relative error of at most 0.0063.
Values may be sent and summed in bfloat16 or wider, within the bound.
No kernel may reach another device: no remote copies, remote signals or barrier semaphores. Data moves between devices by JAX's collectives and lax.ppermute only.
A program may use at most 64 MiB of HBM per device.

v0:
```python
import math

import jax
import jax.numpy as jnp
from jax import lax
from jax.sharding import PartitionSpec as P

RAMP = 8


def build_table(freq_bins, samples):
    sample_ids = jnp.arange(samples, dtype=jnp.int32)
    phase = (freq_bins[:, None] * sample_ids[None, :] % samples).astype(jnp.float32) * jnp.float32(
        2.0 * math.pi / samples
    )
    factor = jnp.float32(1.0 / math.sqrt(samples))
    return jnp.concatenate([jnp.cos(phase) * factor, -jnp.sin(phase) * factor], axis=0).astype(
        jnp.bfloat16
    )


def local(traces, mute_index, freq_bins):
    samples = traces.shape[1]
    src_rows = traces.shape[2]
    rcv_cols = traces.shape[3]
    stations = mute_index.shape[0]
    nbins = freq_bins.shape[0]
    tile_count = lax.axis_size("tile")
    per_tile = nbins // tile_count
    row_first = lax.axis_index("tile") * src_rows
    col_first = lax.axis_index("sub") * rcv_cols
    reflected = jnp.concatenate([mute_index[:0:-1], mute_index])
    starts = col_first - row_first + stations - 1 - jnp.arange(src_rows, dtype=jnp.int32)
    onsets = jax.vmap(lambda first: lax.dynamic_slice_in_dim(reflected, first, rcv_cols))(starts)
    sample_ids = jnp.arange(samples, dtype=jnp.int32)[:, None, None]
    ramp_pos = jnp.clip(
        (sample_ids - onsets[None] + 1).astype(jnp.float32) / jnp.float32(RAMP + 1), 0.0, 1.0
    )
    weights = 0.5 - 0.5 * jnp.cos(jnp.float32(math.pi) * ramp_pos)
    tapered = (traces[0].astype(jnp.float32) * weights).astype(jnp.bfloat16)
    dft_table = build_table(freq_bins, samples)
    spectra = jnp.dot(
        dft_table, tapered.reshape(samples, src_rows * rcv_cols), preferred_element_type=jnp.float32
    )
    spectra = spectra.astype(jnp.bfloat16).reshape(2, nbins, src_rows, rcv_cols)
    arrived = lax.all_to_all(spectra, "tile", split_axis=1, concat_axis=2, tiled=True)
    gathered = lax.all_gather(arrived, "sub", axis=3, tiled=True)
    symmetric = (
        (gathered.astype(jnp.float32) + jnp.swapaxes(gathered, 2, 3).astype(jnp.float32)) * 0.5
    ).astype(jnp.bfloat16)
    columns = lax.dynamic_slice_in_dim(symmetric, col_first, rcv_cols, 3)
    upper_block = jnp.concatenate([columns[0], columns[1]], axis=2)
    lower_block = jnp.concatenate([-columns[1], columns[0]], axis=2)
    right_block = jnp.concatenate([upper_block, lower_block], axis=1)
    factor = jnp.float32(1.0 / math.sqrt(stations))
    line_rows = stations // lax.axis_size("line")
    left_rows = jnp.concatenate([symmetric[0], symmetric[1]], axis=2)
    result = jnp.einsum("bik,bkj->ibj", left_rows, right_block, preferred_element_type=jnp.float32)
    summed = lax.psum_scatter(
        (result * factor).reshape(lax.axis_size("line") * line_rows, per_tile, 2, rcv_cols),
        "line",
        scatter_dimension=0,
        tiled=True,
    )
    return summed.transpose(2, 1, 0, 3)


def solution(mesh):
    return jax.shard_map(
        local,
        mesh=mesh,
        in_specs=(P(("groups", "line"), None, "tile", "sub"), P(), P()),
        out_specs=P(None, "tile", ("groups", "line"), "sub"),
        check_vma=False,
    )
```

profile of v0, /device:TPU:0, one launch (start us, length us, event | category | flops | bytes accessed | tf_op | source)
XLA Modules:
  0.0 696.5 jit_solution(6776162418507956015)
XLA Ops:
  8.2 380.5 %while.1 = (s32[]{:T(128)}, s32[2047]{0:T(1024)S(1)}, s32[256,1]{0,1:T(1,128)S(1)}, s32[256,512]{1,0:T(8,128)S(1)}, s32[]{:T(128)}, /*index=5*/s32[]{:T(128)}) while((s32[]{:T(128)}, s32[2047]{0:T(1024)S(1)}, s32[256,1]{0,1:T(1,128)S(1)}, s32[256,512]{1,0:T(8,128)S(1)}, s32[]{:T(128)}, /*index=5*/s32[]{:T(128)}) %tuple.18), condition=%wide.while_cond, body=%wide.while_body.sunk | while | flops 2 | bytes 8281 | solution.py:34
  10.4 0.8 dynamic-slice.10
  17.8 0.8 dynamic-slice.10
  25.2 0.8 dynamic-slice.10
  38.6 0.8 dynamic-slice.10
  46.0 0.8 dynamic-slice.10
  53.5 0.8 dynamic-slice.10
  66.8 0.8 dynamic-slice.10
  74.3 0.8 dynamic-slice.10
  81.7 0.8 dynamic-slice.10
  95.1 0.8 dynamic-slice.10
  102.5 0.8 dynamic-slice.10
  110.0 0.8 dynamic-slice.10
  123.3 0.8 dynamic-slice.10
  130.8 0.8 dynamic-slice.10
  138.2 0.8 dynamic-slice.10
  151.6 0.8 dynamic-slice.10
  159.0 0.8 dynamic-slice.10
  166.4 0.8 dynamic-slice.10
  179.8 0.8 dynamic-slice.10
  187.2 0.8 dynamic-slice.10
  194.7 0.8 dynamic-slice.10
  208.0 0.8 dynamic-slice.10
  215.5 0.8 dynamic-slice.10
  222.9 0.8 dynamic-slice.10
  236.3 0.8 dynamic-slice.10
  243.7 0.8 dynamic-slice.10
  251.2 0.8 dynamic-slice.10
  264.5 0.8 dynamic-slice.10
  272.0 0.8 dynamic-slice.10
  279.4 0.8 dynamic-slice.10
  292.8 0.8 dynamic-slice.10
  300.2 0.8 dynamic-slice.10
  307.6 0.8 dynamic-slice.10
  321.0 0.8 dynamic-slice.10
  328.4 0.8 dynamic-slice.10
  335.9 0.8 dynamic-slice.10
  388.9 0.8 multiply_convert_fusion.3
  389.6 14.7 %copy.17 = f32[8,8,256,512]{3,1,2,0:T(8,128)S(1)} copy(bf16[8,8,256,512]{3,2,1,0:T(8,128)(2,1)} %bitcast.53) | data formatting | bytes 50331648
  404.3 133.8 %convolution_convert_fusion = bf16[8,131072]{1,0:T(8,128)(2,1)S(1)} fusion(f32[64,131072]{1,0:T(8,128)S(1)} %bitcast.51, s32[131072]{0:T(1024)S(1)} %bitcast.59, bf16[4,64]{1,0:T(4,128)(2,1)S(1)} %get-tuple-element.24, bf16[4,64]{1,0:T(4,128)(2,1)S(1)} %get-tuple-element.23), kind=kOutput, calls=%fused_computation.1 | convolution fusion | flops 219154432 | bytes 36176896 | tf_op jit(solution)/shard_map/dot_general | solution.py:42
  539.0 54.3 %all_to_all.12 = bf16[2,4,256,512]{3,2,0,1:T(8,128)(2,1)S(1)} all-to-all(bf16[2,4,256,512]{3,2,0,1:T(8,128)(2,1)S(1)} %copy.11), channel_id=1, replica_groups=mesh['groups'=2,'tile'=4,'line'=2,'sub'=2] {'tile'}, dimensions={1} | all-to-all | bytes 4194304 | tf_op jit(solution)/shard_map/all_to_all | solution.py:46
  593.3 1.5 copy.12
  594.9 13.0 %all-gather.2.cloned.1.call-done = bf16[2,1,1024,1024]{3,2,0,1:T(8,128)(2,1)} async-done(((bf16[2,1,1024,512]{3,2,0,1:T(8,128)(2,1)}), bf16[2,1,1024,1024]{3,2,0,1:T(8,128)(2,1)}) %all-gather.2.cloned.1.call-update) | async-done | bytes 4194320 | tf_op jit(solution)/shard_map/all_gather | solution.py:47
  608.0 6.9 copy.13
  614.9 6.2 fusion.1
  622.1 6.5 broadcast_multiply_fusion
  628.5 5.4 copy.16
  634.0 55.7 %reduce-scatter.2.cloned.1.call-done = f32[512,1,2,512]{3,0,1,2:T(8,128)} async-done(((f32[1024,1,2,512]{3,0,1,2:T(8,128)}), f32[512,1,2,512]{3,0,1,2:T(8,128)}) %reduce-scatter.2.cloned.1.call-update) | async-done | bytes 2097168 | tf_op jit(solution)/shard_map/reduce_scatter | solution.py:59
  (750 shorter events, 350.6 us)
Async XLA Ops:
  6.5 601.4 %all-gather.2.cloned.1.call-start = ((), (), s32[]{:S(2)}) async-start(), calls=%async_computation.2 | async-start | bytes 6291456 | tf_op jit(solution)/shard_map/all_gather | solution.py:47
  594.9 94.8 %reduce-scatter.2.cloned.1.call-start = ((), (), s32[]{:S(2)}) async-start(), calls=%async_computation.3 | async-start | bytes 6291456 | tf_op jit(solution)/shard_map/reduce_scatter | solution.py:59
Sparse Core Ops, SparseCore 0:
  595.0 12.8 all-gather.1
  634.1 55.5 reduce-scatter.1
where the time goes:
time: 700 us; the launch traced here: 697 us
  local copies, waits for them, and re-layouts  405 us (58%)
  matrix products  140 us (20%)
  waiting for transfers between devices  68.8 us (10%)
  blocking collectives  54.3 us (8%)
  between operations  13.5 us (2%)
  other arithmetic  8.09 us (1%)
    gather x768, local copies, waits for them, and re-layouts  374 us
    dot_general x1, matrix products, local(): jnp.dot(dft_table, tapered.reshape(samples, src_rows * rcv_cols), preferr...  134 us
    reduce_scatter x1, waiting for transfers between devices, local(): lax.psum_scatter((result * factor).reshape(lax.axis_size('line') * line_r...  55.7 us
    all_to_all x1, blocking collectives, local(): lax.all_to_all(spectra, 'tile', split_axis=1, concat_axis=2, tiled=True)  54.3 us
    unnamed x5, local copies, waits for them, and re-layouts  15.7 us
  transfers between devices with their start and end apart: 2, of which 2 were waited for; matrix products, arithmetic and copies ran while one was open for 0% of the time, Pallas kernels for 0%

commit v1 on v0

v1 whole, which is shorter than its diff:
```python
import functools
import math

import jax
import jax.numpy as jnp
from jax import lax
from jax.experimental import pallas as pl
from jax.experimental.pallas import tpu as pltpu
from jax.sharding import PartitionSpec as P

RAMP = 8
LATEST = 15
LANES = 128
GROUP = 16
VMEM_BYTES = 56 * 2**20


def wave_tables(samples):
    phase = jnp.arange(LANES, dtype=jnp.int32) % samples
    phase = phase.astype(jnp.float32) * jnp.float32(2.0 * math.pi / samples)
    factor = jnp.float32(1.0 / math.sqrt(samples))
    return jnp.stack([jnp.cos(phase) * factor, -jnp.sin(phase) * factor])


def ramp_table():
    pos = jnp.clip(jnp.arange(LANES, dtype=jnp.float32) / jnp.float32(RAMP + 1), 0.0, 1.0)
    return (0.5 - 0.5 * jnp.cos(jnp.float32(math.pi) * pos))[None, :]


def ids(shape, axis):
    return lax.broadcasted_iota(jnp.int32, shape, axis)


def spread_table(bins_ref, place, waves_ref, samples, slots):
    rows = slots * 2 * GROUP
    wave = jnp.broadcast_to(waves_ref[0:1, :], (GROUP, LANES))
    other = jnp.broadcast_to(waves_ref[1:2, :], (GROUP, LANES))
    sample = ids((GROUP, LANES), 1)
    lines = []
    for d in range(slots):
        at = place + d
        at = jnp.where(at >= slots, at - slots, at)
        phase = (bins_ref[at] * sample) % samples
        lines.append(jnp.take_along_axis(wave, phase, axis=1))
        lines.append(jnp.take_along_axis(other, phase, axis=1))
    table = jnp.concatenate(lines, axis=0).astype(jnp.bfloat16)[:, :samples]
    wide = samples * GROUP
    pick = ids((samples, wide), 1) // GROUP == ids((samples, wide), 0)
    spread = jnp.dot(table, pick.astype(jnp.bfloat16), preferred_element_type=jnp.float32)
    keep = ids((rows, wide), 0) % GROUP == ids((rows, wide), 1) % GROUP
    return jnp.where(keep, spread, 0.0).astype(jnp.bfloat16)


def onset_window(start, mute_ref, wide):
    parts = mute_ref.shape[0]
    flip = ids((LANES, LANES), 0) + ids((LANES, LANES), 1) == LANES - 1
    mute = mute_ref[...].astype(jnp.float32)
    back = jnp.dot(
        mute.astype(jnp.bfloat16), flip.astype(jnp.bfloat16), preferred_element_type=jnp.float32
    )
    stations = parts * LANES
    tall = 8
    behind = [jnp.broadcast_to(back[i : i + 1, :], (tall, LANES)) for i in reversed(range(parts))]
    ahead = [jnp.broadcast_to(mute[i : i + 1, :], (tall, LANES)) for i in range(parts)]
    behind = pltpu.roll(jnp.concatenate(behind, axis=1), 1, 1)
    both = jnp.concatenate([behind] + ahead, axis=1)
    return pltpu.roll(both, 2 * stations - start, 1)[:, :wide].astype(jnp.int32)


def dft_kernel(
    tapered, base, rows, scalars_ref, bins_ref, x_ref, mute_ref, ramp_ref, waves_ref, *refs
):
    outs, (window_ref, onset_ref, table_ref) = refs[:-3], refs[-3:]
    samples = x_ref.shape[0]
    wide = window_ref.shape[1]
    step = pl.program_id(0)

    @pl.when(step == 0)
    def _():
        window_ref[...] = onset_window(scalars_ref[0], mute_ref, wide)
        table_ref[...] = spread_table(bins_ref, scalars_ref[1], waves_ref, samples, len(outs))

    window = jnp.broadcast_to(window_ref[0:1, :], (rows, wide))
    slanted = pltpu.roll(window, base, 1, stride=1, stride_axis=0)
    onset_ref[...] = pltpu.roll(slanted, step * rows, 1)[:, 0:LANES]
    ramp = jnp.broadcast_to(ramp_ref[0:1, :], (GROUP, LANES))
    for g in range(0, rows, 2 * GROUP):
        halves = []
        for s in (g, g + GROUP):
            onset = onset_ref[s : s + GROUP, :]
            parts = []
            for t in range(samples):
                x = x_ref[t, s : s + GROUP, :]
                if t < tapered:
                    at = jnp.clip(t + 1 - onset, 0, RAMP + 1)
                    weight = jnp.take_along_axis(ramp, at, axis=1)
                    x = (x.astype(jnp.float32) * weight).astype(jnp.bfloat16)
                parts.append(x)
            halves.append(jnp.concatenate(parts, axis=0))
        spectra = jnp.dot(
            table_ref[...], jnp.concatenate(halves, axis=1), preferred_element_type=jnp.float32
        ).astype(jnp.bfloat16)
        for d in range(len(outs)):
            for c in range(2):
                at = (d * 2 + c) * GROUP
                for i in range(2):
                    outs[d][c, g + i * GROUP : g + (i + 1) * GROUP, :] = spectra[
                        at : at + GROUP, i * LANES : (i + 1) * LANES
                    ]


def dft(scalars, bins, traces, mute, ramp, waves, chunk, slots, rows=64):
    samples, src_rows, rcv_cols = traces.shape
    rows = min(rows, src_rows)
    wide = -(-(src_rows + rcv_cols) // LANES) * LANES
    base = wide - src_rows - chunk * LANES
    tapered = min(samples, LATEST + RAMP)
    whole = lambda i, *_: (0, 0)
    return pl.pallas_call(
        functools.partial(dft_kernel, tapered, base, rows),
        grid_spec=pltpu.PrefetchScalarGridSpec(
            num_scalar_prefetch=2,
            grid=(src_rows // rows,),
            in_specs=[
                pl.BlockSpec((samples, rows, LANES), lambda i, *_: (0, i, chunk)),
                pl.BlockSpec(mute.shape, whole),
                pl.BlockSpec(ramp.shape, whole),
                pl.BlockSpec(waves.shape, whole),
            ],
            out_specs=[pl.BlockSpec((2, rows, LANES), lambda i, *_: (0, i, 0))] * slots,
            scratch_shapes=[
                pltpu.VMEM((8, wide), jnp.int32),
                pltpu.VMEM((rows, LANES), jnp.int32),
                pltpu.VMEM((slots * 2 * GROUP, samples * GROUP), jnp.bfloat16),
            ],
        ),
        out_shape=[jax.ShapeDtypeStruct((2, src_rows, LANES), jnp.bfloat16)] * slots,
        compiler_params=pltpu.CompilerParams(vmem_limit_bytes=32 * 2**20),
        cost_estimate=pl.CostEstimate(
            flops=2 * slots * 2 * samples * src_rows * LANES * GROUP,
            bytes_accessed=samples * src_rows * LANES * 2,
            transcendentals=0,
        ),
    )(scalars, bins, traces, mute, ramp, waves)


def collect_kernel(place_ref, *refs):
    blocks, out_ref = refs[:-1], refs[-1]
    slots = len(blocks)
    rows = blocks[0].shape[1]
    for d, block in enumerate(blocks):
        owner = place_ref[0] - d
        owner = jnp.where(owner < 0, owner + slots, owner)
        out_ref[:, pl.ds(pl.multiple_of(owner * rows, rows), rows), :] = block[...]


def collect(place, blocks):
    comps, rows, cols = blocks[0].shape
    vmem = pl.BlockSpec(memory_space=pltpu.VMEM)
    size = len(blocks) * comps * rows * cols
    return pl.pallas_call(
        collect_kernel,
        in_specs=[pl.BlockSpec(memory_space=pltpu.SMEM)] + [vmem] * len(blocks),
        out_specs=vmem,
        out_shape=jax.ShapeDtypeStruct((comps, len(blocks) * rows, cols), jnp.bfloat16),
        compiler_params=pltpu.CompilerParams(vmem_limit_bytes=16 * 2**20),
        cost_estimate=pl.CostEstimate(flops=size, bytes_accessed=4 * size, transcendentals=0),
    )(place, *blocks)


def square_kernel(lines, half, part, scalars_ref, *refs):
    blocks, (out_ref, sym_ref) = refs[:-2], refs[-2:]
    per_line = len(blocks) // lines
    stations = blocks[0].shape[1]
    first, row_at = scalars_ref[0], scalars_ref[1]
    here = first * half
    there = half - here

    def start(a):
        inner = a * LANES
        at = here + inner if inner < half else there + inner - half
        return pl.multiple_of(at, LANES)

    for line in range(lines):
        cols = blocks[line * per_line : (line + 1) * per_line]

        @pl.loop(0, 2)
        def _(c):
            for a in range(per_line):
                for b in range(a, per_line):
                    upper = cols[b][c, pl.ds(start(a), LANES), :].astype(jnp.float32)
                    lower = cols[a][c, pl.ds(start(b), LANES), :].astype(jnp.float32)
                    mean = (upper + lower.T) * 0.5
                    i, j = slice(a * LANES, (a + 1) * LANES), slice(b * LANES, (b + 1) * LANES)
                    sym_ref[c, i, j] = mean.astype(jnp.bfloat16)
                    if a != b:
                        sym_ref[c, j, i] = mean.T.astype(jnp.bfloat16)

        rows = pl.ds(pl.multiple_of(row_at, part), part)
        real_left, imag_left = sym_ref[0, rows, :], sym_ref[1, rows, :]
        real_right, imag_right = sym_ref[0, :, 0:half], sym_ref[1, :, 0:half]
        dot = functools.partial(jnp.dot, preferred_element_type=jnp.float32)
        real = dot(real_left, real_right) - dot(imag_left, imag_right)
        imag = dot(real_left, imag_right) + dot(imag_left, real_right)
        factor = jnp.float32(1.0 / math.sqrt(stations))
        if line == 0:
            out_ref[0, 0], out_ref[1, 0] = real * factor, imag * factor
        else:
            out_ref[0, 0] += real * factor
            out_ref[1, 0] += imag * factor


def square(scalars, blocks, lines, half):
    comps, stations, _ = blocks[0].shape
    part = stations // lines
    vmem = pl.BlockSpec(memory_space=pltpu.VMEM)
    return pl.pallas_call(
        functools.partial(square_kernel, lines, half, part),
        in_specs=[pl.BlockSpec(memory_space=pltpu.SMEM)] + [vmem] * len(blocks),
        out_specs=vmem,
        out_shape=jax.ShapeDtypeStruct((comps, 1, part, half), jnp.float32),
        scratch_shapes=[pltpu.VMEM((comps, stations, stations), jnp.bfloat16)],
        compiler_params=pltpu.CompilerParams(vmem_limit_bytes=VMEM_BYTES),
        cost_estimate=pl.CostEstimate(
            flops=8 * lines * part * half * stations,
            bytes_accessed=4 * lines * stations * stations,
            transcendentals=0,
        ),
    )(scalars, *blocks)


def shift(array, axis, step):
    count = lax.axis_size(axis)
    return lax.ppermute(array, axis, [(i, (i + step) % count) for i in range(count)])


def local(traces, mute_index, freq_bins):
    samples, src_rows, rcv_cols = traces.shape[1:]
    stations = mute_index.shape[0]
    owners, lines = lax.axis_size("tile"), lax.axis_size("line")
    place, side = lax.axis_index("tile"), lax.axis_index("sub")
    mute = mute_index.reshape(stations // LANES, LANES)
    ramp, waves = ramp_table(), wave_tables(samples)
    start = side * rcv_cols - (place + 1) * src_rows + stations
    scalars = jnp.stack([start, place])
    where = place[None]
    chunks = rcv_cols // LANES
    spectra = [
        dft(scalars, freq_bins, traces[0], mute, ramp, waves, m, owners) for m in range(chunks)
    ]
    held = [[[None] * chunks for _ in range(2)] for _ in range(lines)]
    for m in range(chunks):
        arrived = [spectra[m][0]] + [shift(spectra[m][d], "tile", d) for d in range(1, owners)]
        own = collect(where, arrived)
        for e in range(lines):
            passed = shift(own, "line", e) if e else own
            held[e][0][m] = passed
            held[e][1][m] = shift(passed, "sub", 1)
    part = stations // lines
    row = lax.axis_index("line") * part
    row = jnp.where(row // rcv_cols == side, row % rcv_cols, rcv_cols + row % rcv_cols)
    blocks = [block for line in held for owner in line for block in owner]
    return square(jnp.stack([side, row]), blocks, lines, rcv_cols)


def solution(mesh):
    return jax.shard_map(
        local,
        mesh=mesh,
        in_specs=(P(("groups", "line"), None, "tile", "sub"), P(), P()),
        out_specs=P(None, "tile", ("groups", "line"), "sub"),
        check_vma=False,
    )
```

time: 700 us -> 121 us (0.17)
  local copies, waits for them, and re-layouts: 405 us -> 7.15 us
  matrix products: 140 us -> 0 us
  blocking collectives: 54.3 us -> 0 us
  Pallas kernels: 0 us -> 36.5 us
  starting transfers between devices: 0.04 us -> 33.1 us
  waiting for transfers between devices: 68.8 us -> 41.1 us
  between operations: 13.5 us -> 0.25 us
  other arithmetic: 8.09 us -> 0.76 us
    gather x768 -> x0, local copies, waits for them, and re-layouts: 374 us -> none
    dot_general x2 -> x0, matrix products: 140 us -> none  [the longest x1 134 us: local(): jnp.dot(dft_table, tapered.reshape(samples, src_rows * rcv_cols), preferr...]
    reduce_scatter x1 -> x0, waiting for transfers between devices: 55.7 us -> none  [local(): lax.psum_scatter((result * factor).reshape(lax.axis_size('line') * line_r...]
    all_to_all x1 -> x0, blocking collectives: 54.3 us -> none  [local(): lax.all_to_all(spectra, 'tile', split_axis=1, concat_axis=2, tiled=True)]
    ppermute x0 -> x24, waiting for transfers between devices: none -> 41.1 us  [shift(): lax.ppermute(array, axis, [(i, (i + step) % count) for i in range(count)])]
    pallas_call x0 -> x9, Pallas kernels: none -> 36.5 us  [the longest x4 24 us: dft(): pl.pallas_call(functools.partial(dft_kernel, tapered, base, rows), grid_s...]
    ppermute x0 -> x24, starting transfers between devices: none -> 33.1 us  [shift(): lax.ppermute(array, axis, [(i, (i + step) % count) for i in range(count)])]
    all_gather x1 -> x0, waiting for transfers between devices: 13 us -> none  [local(): gathered = lax.all_gather(arrived, 'sub', axis=3, tiled=True)]
  transfers between devices with their start and end apart: 2 -> 24, of which waited for: 2 -> 8; matrix products, arithmetic and copies ran while one was open for 0% -> 0% of each run, Pallas kernels for 0% -> 15%
where the time goes in v1:
time: 121 us; the launch traced here: 119 us
  waiting for transfers between devices  41.1 us (34%)
  Pallas kernels  36.5 us (30%)
  starting transfers between devices  33.1 us (27%)
  local copies, waits for them, and re-layouts  7.15 us (6%)
    ppermute x24, waiting for transfers between devices, shift(): lax.ppermute(array, axis, [(i, (i + step) % count) for i in range(count)])  41.1 us
    ppermute x24, starting transfers between devices, shift(): lax.ppermute(array, axis, [(i, (i + step) % count) for i in range(count)])  33.1 us
    pallas_call x4, Pallas kernels, dft(): pl.pallas_call(functools.partial(dft_kernel, tapered, base, rows), grid_s...  24 us
    pallas_call x1, Pallas kernels, square(): pl.pallas_call(functools.partial(square_kernel, lines, half, part), in_sp...  12.3 us
    unnamed x24, local copies, waits for them, and re-layouts  7.15 us
  transfers between devices with their start and end apart: 24, of which 8 were waited for; matrix products, arithmetic and copies ran while one was open for 0% of the time, Pallas kernels for 15%

profile of v1, /device:TPU:0, one launch (start us, length us, event | category | flops | bytes accessed | tf_op | source)
XLA Modules:
  0.0 118.8 jit_solution(3701449013447782235)
XLA Ops:
  0.0 0.1 multiply_subtract_fusion.ramp_ref
  0.1 0.1 pad_add_fusion.1.scalars_ref
  0.2 5.8 %copy-done = bf16[1,64,256,512]{3,2,1,0:T(8,128)(2,1)S(1)} copy-done((bf16[1,64,256,512]{3,2,1,0:T(8,128)(2,1)S(1)}, bf16[1,64,256,512]{3,2,1,0:T(8,128)(2,1)}, u32[]{:S(2)}) %copy-start) | copy-done | bytes 16777240
  6.0 0.7 copy-done.5
  6.7 0.7 copy-done.6
  7.3 6.0 %shard_map.37 = (bf16[2,256,128]{2,1,0:T(8,128)(2,1)S(1)}, bf16[2,256,128]{2,1,0:T(8,128)(2,1)S(1)}, bf16[2,256,128]{2,1,0:T(8,128)(2,1)S(1)}, bf16[2,256,128]{2,1,0:T(8,128)(2,1)S(1)}) custom-call(s32[2]{0:T(128)S(1)} %pad_add_fusion.1.scalars_ref, s32[4]{0:T(128)S(1)} %copy-done.6, bf16[64,256,512]{2,1,0:T(8,128)(2,1)S(1)} %bitcast.6, ...), custom_call_target="tpu_custom_call" | custom-call | flops 536870912 | bytes 4194304 | tf_op jit(solution)/shard_map/pallas_call | solution.py:119
  13.3 3.1 %collective-permute-start = (bf16[2,256,128]{2,1,0:T(8,128)(2,1)S(1)}, bf16[2,256,128]{2,1,0:T(8,128)(2,1)S(1)}, u32[]{:S(2)}, u32[]{:S(2)}) collective-permute-start(bf16[2,256,128]{2,1,0:T(8,128)(2,1)S(1)} %get-tuple-element.22), channel_id=1, source_target_pairs={{0,4},{4,8},{8,12},{12,0},{1,5},{5,9},{9,13},{13,1},{2,6},{6,10},{... | collective-permute-start | bytes 393224 | tf_op jit(solution)/shard_map/ppermute | solution.py:234
  16.4 2.6 %collective-permute-start.1 = (bf16[2,256,128]{2,1,0:T(8,128)(2,1)S(1)}, bf16[2,256,128]{2,1,0:T(8,128)(2,1)S(1)}, u32[]{:S(2)}, u32[]{:S(2)}) collective-permute-start(bf16[2,256,128]{2,1,0:T(8,128)(2,1)S(1)} %get-tuple-element.23), channel_id=1, source_target_pairs={{0,8},{4,12},{8,0},{12,4},{1,9},{5,13},{9,1},{13,5},{2,10},{6,14},... | collective-permute-start | bytes 393224 | tf_op jit(solution)/shard_map/ppermute | solution.py:234
  19.0 1.3 %collective-permute-start.2 = (bf16[2,256,128]{2,1,0:T(8,128)(2,1)S(1)}, bf16[2,256,128]{2,1,0:T(8,128)(2,1)S(1)}, u32[]{:S(2)}, u32[]{:S(2)}) collective-permute-start(bf16[2,256,128]{2,1,0:T(8,128)(2,1)S(1)} %get-tuple-element.24), channel_id=1, source_target_pairs={{0,12},{4,0},{8,4},{12,8},{1,13},{5,1},{9,5},{13,9},{2,14},{6,2},{... | collective-permute-start | bytes 393224 | tf_op jit(solution)/shard_map/ppermute | solution.py:234
  20.4 2.5 %collective-permute-done.refs_1_ = bf16[2,256,128]{2,1,0:T(8,128)(2,1)S(1)} collective-permute-done((bf16[2,256,128]{2,1,0:T(8,128)(2,1)S(1)}, bf16[2,256,128]{2,1,0:T(8,128)(2,1)S(1)}, u32[]{:S(2)}, u32[]{:S(2)}) %collective-permute-start) | collective-permute-done | bytes 131104 | tf_op jit(solution)/shard_map/ppermute | solution.py:234
  22.9 4.8 %collective-permute-done.1.refs_2_ = bf16[2,256,128]{2,1,0:T(8,128)(2,1)S(1)} collective-permute-done((bf16[2,256,128]{2,1,0:T(8,128)(2,1)S(1)}, bf16[2,256,128]{2,1,0:T(8,128)(2,1)S(1)}, u32[]{:S(2)}, u32[]{:S(2)}) %collective-permute-start.1) | collective-permute-done | bytes 131104 | tf_op jit(solution)/shard_map/ppermute | solution.py:234
  27.7 1.6 %collective-permute-start.16 = (bf16[2,1024,128]{2,1,0:T(8,128)(2,1)S(1)}, bf16[2,1024,128]{2,1,0:T(8,128)(2,1)S(1)}, u32[]{:S(2)}, u32[]{:S(2)}) collective-permute-start(bf16[2,1024,128]{2,1,0:T(8,128)(2,1)S(1)} %shard_map.38.refs_0_), channel_id=1, source_target_pairs={{0,2},{2,0},{1,3},{3,1},{4,6},{6,4},{5,7},{7,5},{8,10},{10,8},{9,1... | collective-permute-start | bytes 1572872 | tf_op jit(solution)/shard_map/ppermute | solution.py:234
  29.3 0.0 collective-permute-start.12
  29.3 6.0 %shard_map.41 = (bf16[2,256,128]{2,1,0:T(8,128)(2,1)S(1)}, bf16[2,256,128]{2,1,0:T(8,128)(2,1)S(1)}, bf16[2,256,128]{2,1,0:T(8,128)(2,1)S(1)}, bf16[2,256,128]{2,1,0:T(8,128)(2,1)S(1)}) custom-call(s32[2]{0:T(128)S(1)} %pad_add_fusion.1.scalars_ref, s32[4]{0:T(128)S(1)} %copy-done.6, bf16[64,256,512]{2,1,0:T(8,128)(2,1)S(1)} %bitcast.7, ...), custom_call_target="tpu_custom_call" | custom-call | flops 536870912 | bytes 4194304 | tf_op jit(solution)/shard_map/pallas_call | solution.py:119
  35.3 3.3 %collective-permute-start.6 = (bf16[2,256,128]{2,1,0:T(8,128)(2,1)S(1)}, bf16[2,256,128]{2,1,0:T(8,128)(2,1)S(1)}, u32[]{:S(2)}, u32[]{:S(2)}) collective-permute-start(bf16[2,256,128]{2,1,0:T(8,128)(2,1)S(1)} %get-tuple-element.30), channel_id=1, source_target_pairs={{0,4},{4,8},{8,12},{12,0},{1,5},{5,9},{9,13},{13,1},{2,6},{6,10},{... | collective-permute-start | bytes 393224 | tf_op jit(solution)/shard_map/ppermute | solution.py:234
  38.6 1.6 %collective-permute-start.7 = (bf16[2,256,128]{2,1,0:T(8,128)(2,1)S(1)}, bf16[2,256,128]{2,1,0:T(8,128)(2,1)S(1)}, u32[]{:S(2)}, u32[]{:S(2)}) collective-permute-start(bf16[2,256,128]{2,1,0:T(8,128)(2,1)S(1)} %get-tuple-element.31), channel_id=1, source_target_pairs={{0,8},{4,12},{8,0},{12,4},{1,9},{5,13},{9,1},{13,5},{2,10},{6,14},... | collective-permute-start | bytes 393224 | tf_op jit(solution)/shard_map/ppermute | solution.py:234
  40.2 0.8 collective-permute-start.8
  41.0 6.0 %shard_map.39 = (bf16[2,256,128]{2,1,0:T(8,128)(2,1)S(1)}, bf16[2,256,128]{2,1,0:T(8,128)(2,1)S(1)}, bf16[2,256,128]{2,1,0:T(8,128)(2,1)S(1)}, bf16[2,256,128]{2,1,0:T(8,128)(2,1)S(1)}) custom-call(s32[2]{0:T(128)S(1)} %pad_add_fusion.1.scalars_ref, s32[4]{0:T(128)S(1)} %copy-done.6, bf16[64,256,512]{2,1,0:T(8,128)(2,1)S(1)} %bitcast.8, ...), custom_call_target="tpu_custom_call" | custom-call | flops 536870912 | bytes 4194304 | tf_op jit(solution)/shard_map/pallas_call | solution.py:119
  47.0 0.0 collective-permute-done.6.refs_1_
  47.1 1.3 %collective-permute-start.3 = (bf16[2,256,128]{2,1,0:T(8,128)(2,1)S(1)}, bf16[2,256,128]{2,1,0:T(8,128)(2,1)S(1)}, u32[]{:S(2)}, u32[]{:S(2)}) collective-permute-start(bf16[2,256,128]{2,1,0:T(8,128)(2,1)S(1)} %get-tuple-element.26), channel_id=1, source_target_pairs={{0,4},{4,8},{8,12},{12,0},{1,5},{5,9},{9,13},{13,1},{2,6},{6,10},{... | collective-permute-start | bytes 393224 | tf_op jit(solution)/shard_map/ppermute | solution.py:234
  48.3 1.2 collective-permute-done.7.refs_2_
  49.5 0.1 collective-permute-start.4
  49.6 0.0 collective-permute-done.8.refs_3_
  49.6 4.2 %collective-permute-start.5 = (bf16[2,256,128]{2,1,0:T(8,128)(2,1)S(1)}, bf16[2,256,128]{2,1,0:T(8,128)(2,1)S(1)}, u32[]{:S(2)}, u32[]{:S(2)}) collective-permute-start(bf16[2,256,128]{2,1,0:T(8,128)(2,1)S(1)} %get-tuple-element.28), channel_id=1, source_target_pairs={{0,12},{4,0},{8,4},{12,8},{1,13},{5,1},{9,5},{13,9},{2,14},{6,2},{... | collective-permute-start | bytes 393224 | tf_op jit(solution)/shard_map/ppermute | solution.py:234
  53.8 6.0 %shard_map.43 = (bf16[2,256,128]{2,1,0:T(8,128)(2,1)S(1)}, bf16[2,256,128]{2,1,0:T(8,128)(2,1)S(1)}, bf16[2,256,128]{2,1,0:T(8,128)(2,1)S(1)}, bf16[2,256,128]{2,1,0:T(8,128)(2,1)S(1)}) custom-call(s32[2]{0:T(128)S(1)} %pad_add_fusion.1.scalars_ref, s32[4]{0:T(128)S(1)} %copy-done.6, bf16[64,256,512]{2,1,0:T(8,128)(2,1)S(1)} %bitcast.9, ...), custom_call_target="tpu_custom_call" | custom-call | flops 536870912 | bytes 4194304 | tf_op jit(solution)/shard_map/pallas_call | solution.py:119
  59.8 4.8 %collective-permute-start.9 = (bf16[2,256,128]{2,1,0:T(8,128)(2,1)S(1)}, bf16[2,256,128]{2,1,0:T(8,128)(2,1)S(1)}, u32[]{:S(2)}, u32[]{:S(2)}) collective-permute-start(bf16[2,256,128]{2,1,0:T(8,128)(2,1)S(1)} %get-tuple-element.34), channel_id=1, source_target_pairs={{0,4},{4,8},{8,12},{12,0},{1,5},{5,9},{9,13},{13,1},{2,6},{6,10},{... | collective-permute-start | bytes 393224 | tf_op jit(solution)/shard_map/ppermute | solution.py:234
  64.6 0.0 collective-permute-done.4.refs_2_
  64.6 1.5 %collective-permute-start.10 = (bf16[2,256,128]{2,1,0:T(8,128)(2,1)S(1)}, bf16[2,256,128]{2,1,0:T(8,128)(2,1)S(1)}, u32[]{:S(2)}, u32[]{:S(2)}) collective-permute-start(bf16[2,256,128]{2,1,0:T(8,128)(2,1)S(1)} %get-tuple-element.35), channel_id=1, source_target_pairs={{0,8},{4,12},{8,0},{12,4},{1,9},{5,13},{9,1},{13,5},{2,10},{6,14},... | collective-permute-start | bytes 393224 | tf_op jit(solution)/shard_map/ppermute | solution.py:234
  66.1 2.8 %collective-permute-start.11 = (bf16[2,256,128]{2,1,0:T(8,128)(2,1)S(1)}, bf16[2,256,128]{2,1,0:T(8,128)(2,1)S(1)}, u32[]{:S(2)}, u32[]{:S(2)}) collective-permute-start(bf16[2,256,128]{2,1,0:T(8,128)(2,1)S(1)} %get-tuple-element.36), channel_id=1, source_target_pairs={{0,12},{4,0},{8,4},{12,8},{1,13},{5,1},{9,5},{13,9},{2,14},{6,2},{... | collective-permute-start | bytes 393224 | tf_op jit(solution)/shard_map/ppermute | solution.py:234
  69.1 0.0 collective-permute-done.9.refs_1_
  69.1 0.6 collective-permute-start.17
  69.7 5.0 %collective-permute-done.10.refs_2_ = bf16[2,256,128]{2,1,0:T(8,128)(2,1)S(1)} collective-permute-done((bf16[2,256,128]{2,1,0:T(8,128)(2,1)S(1)}, bf16[2,256,128]{2,1,0:T(8,128)(2,1)S(1)}, u32[]{:S(2)}, u32[]{:S(2)}) %collective-permute-start.10) | collective-permute-done | bytes 131104 | tf_op jit(solution)/shard_map/ppermute | solution.py:234
  74.7 0.0 collective-permute-start.13
  74.7 0.0 collective-permute-done.11.refs_3_
  74.7 0.5 collective-permute-start.18
  75.3 0.0 collective-permute-done.16.refs_8_
  75.3 0.3 collective-permute-start.14
  75.6 0.0 collective-permute-done.12.refs_4_
  75.6 1.5 %collective-permute-start.19 = (bf16[2,1024,128]{2,1,0:T(8,128)(2,1)S(1)}, bf16[2,1024,128]{2,1,0:T(8,128)(2,1)S(1)}, u32[]{:S(2)}, u32[]{:S(2)}) collective-permute-start(bf16[2,1024,128]{2,1,0:T(8,128)(2,1)S(1)} %shard_map.44.refs_3_), channel_id=1, source_target_pairs={{0,2},{2,0},{1,3},{3,1},{4,6},{6,4},{5,7},{7,5},{8,10},{10,8},{9,1... | collective-permute-start | bytes 1572872 | tf_op jit(solution)/shard_map/ppermute | solution.py:234
  77.1 7.0 %collective-permute-done.17.refs_9_ = bf16[2,1024,128]{2,1,0:T(8,128)(2,1)} collective-permute-done((bf16[2,1024,128]{2,1,0:T(8,128)(2,1)S(1)}, bf16[2,1024,128]{2,1,0:T(8,128)(2,1)}, u32[]{:S(2)}, u32[]{:S(2)}) %collective-permute-start.17) | collective-permute-done | bytes 524320 | tf_op jit(solution)/shard_map/ppermute | solution.py:234
  84.1 0.5 collective-permute-start.20
  84.6 10.7 %collective-permute-done.18.refs_10_ = bf16[2,1024,128]{2,1,0:T(8,128)(2,1)} collective-permute-done((bf16[2,1024,128]{2,1,0:T(8,128)(2,1)S(1)}, bf16[2,1024,128]{2,1,0:T(8,128)(2,1)}, u32[]{:S(2)}, u32[]{:S(2)}) %collective-permute-start.18) | collective-permute-done | bytes 524320 | tf_op jit(solution)/shard_map/ppermute | solution.py:234
  95.3 0.5 collective-permute-start.22
  95.8 8.5 %collective-permute-done.19.refs_11_ = bf16[2,1024,128]{2,1,0:T(8,128)(2,1)S(1)} collective-permute-done((bf16[2,1024,128]{2,1,0:T(8,128)(2,1)S(1)}, bf16[2,1024,128]{2,1,0:T(8,128)(2,1)S(1)}, u32[]{:S(2)}, u32[]{:S(2)}) %collective-permute-start.19) | collective-permute-done | bytes 524320 | tf_op jit(solution)/shard_map/ppermute | solution.py:234
  104.3 0.1 collective-permute-start.23
  104.5 0.6 pad_add_fusion.scalars_ref
  105.1 1.4 %collective-permute-done.23.refs_15_ = bf16[2,1024,128]{2,1,0:T(8,128)(2,1)} collective-permute-done((bf16[2,1024,128]{2,1,0:T(8,128)(2,1)S(1)}, bf16[2,1024,128]{2,1,0:T(8,128)(2,1)}, u32[]{:S(2)}, u32[]{:S(2)}) %collective-permute-start.23) | collective-permute-done | bytes 524320 | tf_op jit(solution)/shard_map/ppermute | solution.py:234
  106.5 12.3 %shard_map.45 = f32[2,1,512,512]{3,2,1,0:T(8,128)} custom-call(s32[2]{0:T(128)} %pad_add_fusion.scalars_ref, bf16[2,1024,128]{2,1,0:T(8,128)(2,1)} %copy-done.1, bf16[2,1024,128]{2,1,0:T(8,128)(2,1)} %copy-done.3, bf16[2,1024,128]{2,1,0:T(8,128)(2,1)} %copy-done.2, bf16[2,1024,128]{2,1,0:T(8,128)(2,1)} %copy-done.4, bf16[2,1024,128]{2,1,0:T(8,128)(2,1)} %copy-done.8, ...), custom_call_target="tpu_custom_call" | custom-call | flops 4294967296 | bytes 8388608 | tf_op jit(solution)/shard_map/pallas_call | solution.py:217
  (38 shorter events, 0.3 us)
Async XLA Ops:
  0.2 5.8 %copy-start = (bf16[1,64,256,512]{3,2,1,0:T(8,128)(2,1)S(1)}, bf16[1,64,256,512]{3,2,1,0:T(8,128)(2,1)}, u32[]{:S(2)}) copy-start(bf16[1,64,256,512]{3,2,1,0:T(8,128)(2,1)} %param.3) | copy-start | bytes 50331652
  6.0 0.7 copy-start.5
  6.7 0.7 copy-start.6
  13.3 9.6 %collective-permute-start = (bf16[2,256,128]{2,1,0:T(8,128)(2,1)S(1)}, bf16[2,256,128]{2,1,0:T(8,128)(2,1)S(1)}, u32[]{:S(2)}, u32[]{:S(2)}) collective-permute-start(bf16[2,256,128]{2,1,0:T(8,128)(2,1)S(1)} %get-tuple-element.22), channel_id=1, source_target_pairs={{0,4},{4,8},{8,12},{12,0},{1,5},{5,9},{9,13},{13,1},{2,6},{6,10},{... | collective-permute-start | bytes 393224 | tf_op jit(solution)/shard_map/ppermute | solution.py:234
  16.4 11.2 %collective-permute-start.1 = (bf16[2,256,128]{2,1,0:T(8,128)(2,1)S(1)}, bf16[2,256,128]{2,1,0:T(8,128)(2,1)S(1)}, u32[]{:S(2)}, u32[]{:S(2)}) collective-permute-start(bf16[2,256,128]{2,1,0:T(8,128)(2,1)S(1)} %get-tuple-element.23), channel_id=1, source_target_pairs={{0,8},{4,12},{8,0},{12,4},{1,9},{5,13},{9,1},{13,5},{2,10},{6,14},... | collective-permute-start | bytes 393224 | tf_op jit(solution)/shard_map/ppermute | solution.py:234
  19.0 8.6 %collective-permute-start.2 = (bf16[2,256,128]{2,1,0:T(8,128)(2,1)S(1)}, bf16[2,256,128]{2,1,0:T(8,128)(2,1)S(1)}, u32[]{:S(2)}, u32[]{:S(2)}) collective-permute-start(bf16[2,256,128]{2,1,0:T(8,128)(2,1)S(1)} %get-tuple-element.24), channel_id=1, source_target_pairs={{0,12},{4,0},{8,4},{12,8},{1,13},{5,1},{9,5},{13,9},{2,14},{6,2},{... | collective-permute-start | bytes 393224 | tf_op jit(solution)/shard_map/ppermute | solution.py:234
  27.7 19.3 %copy-start.1 = (bf16[2,1024,128]{2,1,0:T(8,128)(2,1)}, bf16[2,1024,128]{2,1,0:T(8,128)(2,1)S(1)}, u32[]{:S(2)}) copy-start(bf16[2,1024,128]{2,1,0:T(8,128)(2,1)S(1)} %shard_map.38.refs_0_) | copy-start | bytes 1572868
  27.7 47.6 %collective-permute-start.16 = (bf16[2,1024,128]{2,1,0:T(8,128)(2,1)S(1)}, bf16[2,1024,128]{2,1,0:T(8,128)(2,1)S(1)}, u32[]{:S(2)}, u32[]{:S(2)}) collective-permute-start(bf16[2,1024,128]{2,1,0:T(8,128)(2,1)S(1)} %shard_map.38.refs_0_), channel_id=1, source_target_pairs={{0,2},{2,0},{1,3},{3,1},{4,6},{6,4},{5,7},{7,5},{8,10},{10,8},{9,1... | collective-permute-start | bytes 1572872 | tf_op jit(solution)/shard_map/ppermute | solution.py:234
  29.3 46.3 %collective-permute-start.12 = (bf16[2,1024,128]{2,1,0:T(8,128)(2,1)S(1)}, bf16[2,1024,128]{2,1,0:T(8,128)(2,1)S(1)}, u32[]{:S(2)}, u32[]{:S(2)}) collective-permute-start(bf16[2,1024,128]{2,1,0:T(8,128)(2,1)S(1)} %shard_map.38.refs_0_), channel_id=1, source_target_pairs={{0,1},{1,0},{2,3},{3,2},{4,5},{5,4},{6,7},{7,6},{8,9},{9,8},{10,11... | collective-permute-start | bytes 1572872 | tf_op jit(solution)/shard_map/ppermute | solution.py:234
  35.3 11.8 %collective-permute-start.6 = (bf16[2,256,128]{2,1,0:T(8,128)(2,1)S(1)}, bf16[2,256,128]{2,1,0:T(8,128)(2,1)S(1)}, u32[]{:S(2)}, u32[]{:S(2)}) collective-permute-start(bf16[2,256,128]{2,1,0:T(8,128)(2,1)S(1)} %get-tuple-element.30), channel_id=1, source_target_pairs={{0,4},{4,8},{8,12},{12,0},{1,5},{5,9},{9,13},{13,1},{2,6},{6,10},{... | collective-permute-start | bytes 393224 | tf_op jit(solution)/shard_map/ppermute | solution.py:234
  38.6 10.9 %collective-permute-start.7 = (bf16[2,256,128]{2,1,0:T(8,128)(2,1)S(1)}, bf16[2,256,128]{2,1,0:T(8,128)(2,1)S(1)}, u32[]{:S(2)}, u32[]{:S(2)}) collective-permute-start(bf16[2,256,128]{2,1,0:T(8,128)(2,1)S(1)} %get-tuple-element.31), channel_id=1, source_target_pairs={{0,8},{4,12},{8,0},{12,4},{1,9},{5,13},{9,1},{13,5},{2,10},{6,14},... | collective-permute-start | bytes 393224 | tf_op jit(solution)/shard_map/ppermute | solution.py:234
  40.2 9.4 %collective-permute-start.8 = (bf16[2,256,128]{2,1,0:T(8,128)(2,1)S(1)}, bf16[2,256,128]{2,1,0:T(8,128)(2,1)S(1)}, u32[]{:S(2)}, u32[]{:S(2)}) collective-permute-start(bf16[2,256,128]{2,1,0:T(8,128)(2,1)S(1)} %get-tuple-element.32), channel_id=1, source_target_pairs={{0,12},{4,0},{8,4},{12,8},{1,13},{5,1},{9,5},{13,9},{2,14},{6,2},{... | collective-permute-start | bytes 393224 | tf_op jit(solution)/shard_map/ppermute | solution.py:234
  47.1 12.7 %collective-permute-start.3 = (bf16[2,256,128]{2,1,0:T(8,128)(2,1)S(1)}, bf16[2,256,128]{2,1,0:T(8,128)(2,1)S(1)}, u32[]{:S(2)}, u32[]{:S(2)}) collective-permute-start(bf16[2,256,128]{2,1,0:T(8,128)(2,1)S(1)} %get-tuple-element.26), channel_id=1, source_target_pairs={{0,4},{4,8},{8,12},{12,0},{1,5},{5,9},{9,13},{13,1},{2,6},{6,10},{... | collective-permute-start | bytes 393224 | tf_op jit(solution)/shard_map/ppermute | solution.py:234
  49.5 15.1 %collective-permute-start.4 = (bf16[2,256,128]{2,1,0:T(8,128)(2,1)S(1)}, bf16[2,256,128]{2,1,0:T(8,128)(2,1)S(1)}, u32[]{:S(2)}, u32[]{:S(2)}) collective-permute-start(bf16[2,256,128]{2,1,0:T(8,128)(2,1)S(1)} %get-tuple-element.27), channel_id=1, source_target_pairs={{0,8},{4,12},{8,0},{12,4},{1,9},{5,13},{9,1},{13,5},{2,10},{6,14},... | collective-permute-start | bytes 393224 | tf_op jit(solution)/shard_map/ppermute | solution.py:234
  49.6 16.5 %collective-permute-start.5 = (bf16[2,256,128]{2,1,0:T(8,128)(2,1)S(1)}, bf16[2,256,128]{2,1,0:T(8,128)(2,1)S(1)}, u32[]{:S(2)}, u32[]{:S(2)}) collective-permute-start(bf16[2,256,128]{2,1,0:T(8,128)(2,1)S(1)} %get-tuple-element.28), channel_id=1, source_target_pairs={{0,12},{4,0},{8,4},{12,8},{1,13},{5,1},{9,5},{13,9},{2,14},{6,2},{... | collective-permute-start | bytes 393224 | tf_op jit(solution)/shard_map/ppermute | solution.py:234
  59.8 9.3 %collective-permute-start.9 = (bf16[2,256,128]{2,1,0:T(8,128)(2,1)S(1)}, bf16[2,256,128]{2,1,0:T(8,128)(2,1)S(1)}, u32[]{:S(2)}, u32[]{:S(2)}) collective-permute-start(bf16[2,256,128]{2,1,0:T(8,128)(2,1)S(1)} %get-tuple-element.34), channel_id=1, source_target_pairs={{0,4},{4,8},{8,12},{12,0},{1,5},{5,9},{9,13},{13,1},{2,6},{6,10},{... | collective-permute-start | bytes 393224 | tf_op jit(solution)/shard_map/ppermute | solution.py:234
  64.6 10.1 %collective-permute-start.10 = (bf16[2,256,128]{2,1,0:T(8,128)(2,1)S(1)}, bf16[2,256,128]{2,1,0:T(8,128)(2,1)S(1)}, u32[]{:S(2)}, u32[]{:S(2)}) collective-permute-start(bf16[2,256,128]{2,1,0:T(8,128)(2,1)S(1)} %get-tuple-element.35), channel_id=1, source_target_pairs={{0,8},{4,12},{8,0},{12,4},{1,9},{5,13},{9,1},{13,5},{2,10},{6,14},... | collective-permute-start | bytes 393224 | tf_op jit(solution)/shard_map/ppermute | solution.py:234
  66.1 8.5 %collective-permute-start.11 = (bf16[2,256,128]{2,1,0:T(8,128)(2,1)S(1)}, bf16[2,256,128]{2,1,0:T(8,128)(2,1)S(1)}, u32[]{:S(2)}, u32[]{:S(2)}) collective-permute-start(bf16[2,256,128]{2,1,0:T(8,128)(2,1)S(1)} %get-tuple-element.36), channel_id=1, source_target_pairs={{0,12},{4,0},{8,4},{12,8},{1,13},{5,1},{9,5},{13,9},{2,14},{6,2},{... | collective-permute-start | bytes 393224 | tf_op jit(solution)/shard_map/ppermute | solution.py:234
  69.0 37.4 %copy-start.2 = (bf16[2,1024,128]{2,1,0:T(8,128)(2,1)}, bf16[2,1024,128]{2,1,0:T(8,128)(2,1)S(1)}, u32[]{:S(2)}) copy-start(bf16[2,1024,128]{2,1,0:T(8,128)(2,1)S(1)} %shard_map.42.refs_2_) | copy-start | bytes 1572868
  69.1 37.4 %copy-start.3 = (bf16[2,1024,128]{2,1,0:T(8,128)(2,1)}, bf16[2,1024,128]{2,1,0:T(8,128)(2,1)S(1)}, u32[]{:S(2)}) copy-start(bf16[2,1024,128]{2,1,0:T(8,128)(2,1)S(1)} %shard_map.40.refs_1_) | copy-start | bytes 1572868
  69.1 15.0 %collective-permute-start.17 = (bf16[2,1024,128]{2,1,0:T(8,128)(2,1)S(1)}, bf16[2,1024,128]{2,1,0:T(8,128)(2,1)}, u32[]{:S(2)}, u32[]{:S(2)}) collective-permute-start(bf16[2,1024,128]{2,1,0:T(8,128)(2,1)S(1)} %shard_map.40.refs_1_), channel_id=1, source_target_pairs={{0,2},{2,0},{1,3},{3,1},{4,6},{6,4},{5,7},{7,5},{8,10},{10,8},{9,1... | collective-permute-start | bytes 1572872 | tf_op jit(solution)/shard_map/ppermute | solution.py:234
  74.7 9.4 %collective-permute-start.13 = (bf16[2,1024,128]{2,1,0:T(8,128)(2,1)S(1)}, bf16[2,1024,128]{2,1,0:T(8,128)(2,1)S(1)}, u32[]{:S(2)}, u32[]{:S(2)}) collective-permute-start(bf16[2,1024,128]{2,1,0:T(8,128)(2,1)S(1)} %shard_map.40.refs_1_), channel_id=1, source_target_pairs={{0,1},{1,0},{2,3},{3,2},{4,5},{5,4},{6,7},{7,6},{8,9},{9,8},{10,11... | collective-permute-start | bytes 1572872 | tf_op jit(solution)/shard_map/ppermute | solution.py:234
  74.7 20.6 %collective-permute-start.18 = (bf16[2,1024,128]{2,1,0:T(8,128)(2,1)S(1)}, bf16[2,1024,128]{2,1,0:T(8,128)(2,1)}, u32[]{:S(2)}, u32[]{:S(2)}) collective-permute-start(bf16[2,1024,128]{2,1,0:T(8,128)(2,1)S(1)} %shard_map.42.refs_2_), channel_id=1, source_target_pairs={{0,2},{2,0},{1,3},{3,1},{4,6},{6,4},{5,7},{7,5},{8,10},{10,8},{9,1... | collective-permute-start | bytes 1572872 | tf_op jit(solution)/shard_map/ppermute | solution.py:234
  75.3 31.2 %copy-start.4 = (bf16[2,1024,128]{2,1,0:T(8,128)(2,1)}, bf16[2,1024,128]{2,1,0:T(8,128)(2,1)S(1)}, u32[]{:S(2)}) copy-start(bf16[2,1024,128]{2,1,0:T(8,128)(2,1)S(1)} %shard_map.44.refs_3_) | copy-start | bytes 1572868
  75.3 31.2 %copy-start.7 = (bf16[2,1024,128]{2,1,0:T(8,128)(2,1)}, bf16[2,1024,128]{2,1,0:T(8,128)(2,1)S(1)}, u32[]{:S(2)}) copy-start(bf16[2,1024,128]{2,1,0:T(8,128)(2,1)S(1)} %collective-permute-done.16.refs_8_) | copy-start | bytes 1572868
  75.3 20.0 %collective-permute-start.14 = (bf16[2,1024,128]{2,1,0:T(8,128)(2,1)S(1)}, bf16[2,1024,128]{2,1,0:T(8,128)(2,1)S(1)}, u32[]{:S(2)}, u32[]{:S(2)}) collective-permute-start(bf16[2,1024,128]{2,1,0:T(8,128)(2,1)S(1)} %shard_map.42.refs_2_), channel_id=1, source_target_pairs={{0,1},{1,0},{2,3},{3,2},{4,5},{5,4},{6,7},{7,6},{8,9},{9,8},{10,11... | collective-permute-start | bytes 1572872 | tf_op jit(solution)/shard_map/ppermute | solution.py:234
  75.6 30.9 %copy-start.8 = (bf16[2,1024,128]{2,1,0:T(8,128)(2,1)}, bf16[2,1024,128]{2,1,0:T(8,128)(2,1)S(1)}, u32[]{:S(2)}) copy-start(bf16[2,1024,128]{2,1,0:T(8,128)(2,1)S(1)} %collective-permute-done.12.refs_4_) | copy-start | bytes 1572868
  75.6 28.8 %collective-permute-start.19 = (bf16[2,1024,128]{2,1,0:T(8,128)(2,1)S(1)}, bf16[2,1024,128]{2,1,0:T(8,128)(2,1)S(1)}, u32[]{:S(2)}, u32[]{:S(2)}) collective-permute-start(bf16[2,1024,128]{2,1,0:T(8,128)(2,1)S(1)} %shard_map.44.refs_3_), channel_id=1, source_target_pairs={{0,2},{2,0},{1,3},{3,1},{4,6},{6,4},{5,7},{7,5},{8,10},{10,8},{9,1... | collective-permute-start | bytes 1572872 | tf_op jit(solution)/shard_map/ppermute | solution.py:234
  84.1 21.0 %collective-permute-start.15 = (bf16[2,1024,128]{2,1,0:T(8,128)(2,1)S(1)}, bf16[2,1024,128]{2,1,0:T(8,128)(2,1)}, u32[]{:S(2)}, u32[]{:S(2)}) collective-permute-start(bf16[2,1024,128]{2,1,0:T(8,128)(2,1)S(1)} %shard_map.44.refs_3_), channel_id=1, source_target_pairs={{0,1},{1,0},{2,3},{3,2},{4,5},{5,4},{6,7},{7,6},{8,9},{9,8},{10,11... | collective-permute-start | bytes 1572872 | tf_op jit(solution)/shard_map/ppermute | solution.py:234
  84.1 20.3 %copy-start.9 = (bf16[2,1024,128]{2,1,0:T(8,128)(2,1)}, bf16[2,1024,128]{2,1,0:T(8,128)(2,1)S(1)}, u32[]{:S(2)}) copy-start(bf16[2,1024,128]{2,1,0:T(8,128)(2,1)S(1)} %collective-permute-done.13.refs_5_) | copy-start | bytes 1572868
  84.1 20.9 %collective-permute-start.20 = (bf16[2,1024,128]{2,1,0:T(8,128)(2,1)S(1)}, bf16[2,1024,128]{2,1,0:T(8,128)(2,1)}, u32[]{:S(2)}, u32[]{:S(2)}) collective-permute-start(bf16[2,1024,128]{2,1,0:T(8,128)(2,1)S(1)} %collective-permute-done.16.refs_8_), channel_id=1, source_target_pairs={{0,1},{1,0},{2,3},{3,2},{4,5},{5,4},{6,7},{7,6},{8,9},{9,8},{10,11... | collective-permute-start | bytes 1572872 | tf_op jit(solution)/shard_map/ppermute | solution.py:234
  95.3 9.7 %collective-permute-start.21 = (bf16[2,1024,128]{2,1,0:T(8,128)(2,1)}, bf16[2,1024,128]{2,1,0:T(8,128)(2,1)}, u32[]{:S(2)}, u32[]{:S(2)}) collective-permute-start(bf16[2,1024,128]{2,1,0:T(8,128)(2,1)} %collective-permute-done.17.refs_9_), channel_id=1, source_target_pairs={{0,1},{1,0},{2,3},{3,2},{4,5},{5,4},{6,7},{7,6},{8,9},{9,8},{10,11... | collective-permute-start | bytes 1572872 | tf_op jit(solution)/shard_map/ppermute | solution.py:234
  95.3 9.0 %copy-start.10 = (bf16[2,1024,128]{2,1,0:T(8,128)(2,1)}, bf16[2,1024,128]{2,1,0:T(8,128)(2,1)S(1)}, u32[]{:S(2)}) copy-start(bf16[2,1024,128]{2,1,0:T(8,128)(2,1)S(1)} %collective-permute-done.14.refs_6_) | copy-start | bytes 1572868
  95.3 9.7 %collective-permute-start.22 = (bf16[2,1024,128]{2,1,0:T(8,128)(2,1)}, bf16[2,1024,128]{2,1,0:T(8,128)(2,1)}, u32[]{:S(2)}, u32[]{:S(2)}) collective-permute-start(bf16[2,1024,128]{2,1,0:T(8,128)(2,1)} %collective-permute-done.18.refs_10_), channel_id=1, source_target_pairs={{0,1},{1,0},{2,3},{3,2},{4,5},{5,4},{6,7},{7,6},{8,9},{9,8},{10,11... | collective-permute-start | bytes 1572872 | tf_op jit(solution)/shard_map/ppermute | solution.py:234
  104.3 2.1 %copy-start.11 = (bf16[2,1024,128]{2,1,0:T(8,128)(2,1)}, bf16[2,1024,128]{2,1,0:T(8,128)(2,1)S(1)}, u32[]{:S(2)}) copy-start(bf16[2,1024,128]{2,1,0:T(8,128)(2,1)S(1)} %collective-permute-done.19.refs_11_) | copy-start | bytes 1572868
  104.3 2.1 %collective-permute-start.23 = (bf16[2,1024,128]{2,1,0:T(8,128)(2,1)S(1)}, bf16[2,1024,128]{2,1,0:T(8,128)(2,1)}, u32[]{:S(2)}, u32[]{:S(2)}) collective-permute-start(bf16[2,1024,128]{2,1,0:T(8,128)(2,1)S(1)} %collective-permute-done.19.refs_11_), channel_id=1, source_target_pairs={{0,1},{1,0},{2,3},{3,2},{4,5},{5,4},{6,7},{7,6},{8,9},{9,8},{10,11... | collective-permute-start | bytes 1572872 | tf_op jit(solution)/shard_map/ppermute | solution.py:234

commit v2 on v1

v2 whole, which is shorter than its diff:
```python
import functools
import math

import jax
import jax.numpy as jnp
from jax import lax
from jax.experimental import pallas as pl
from jax.experimental.pallas import tpu as pltpu
from jax.sharding import PartitionSpec as P


RAMP = 8
LATEST = 15
LANES = 128
GROUP = 16


def ids(shape, axis):
    return lax.broadcasted_iota(jnp.int32, shape, axis)


def ramp_table():
    pos = (ids((GROUP, LANES), 1) - GROUP).astype(jnp.float32)
    pos = jnp.clip(pos / jnp.float32(RAMP + 1), 0.0, 1.0)
    return 0.5 - 0.5 * jnp.cos(jnp.float32(math.pi) * pos)


def receiver(place, distance, count):
    if count & (count - 1) == 0:
        return place ^ distance, place ^ distance
    return (place + distance) % count, (place - distance) % count


def spread_table(bins_ref, place, samples, slots):
    rows = slots * 2 * GROUP
    bins = jnp.zeros((rows, LANES), jnp.int32)
    row = ids((rows, LANES), 0) // GROUP
    for k in range(slots):
        bins = jnp.where(row // 2 == k, bins_ref[receiver(place, k, slots)[0]], bins)
    phase = (bins * ids((rows, LANES), 1)) % samples
    angle = phase.astype(jnp.float32) * jnp.float32(2.0 * math.pi / samples)
    factor = jnp.float32(1.0 / math.sqrt(samples))
    table = jnp.where(row % 2 == 0, jnp.cos(angle) * factor, -jnp.sin(angle) * factor)
    table = table.astype(jnp.bfloat16)[:, :samples]
    wide = samples * GROUP
    pick = ids((samples, wide), 1) // GROUP == ids((samples, wide), 0)
    spread = jnp.dot(table, pick.astype(jnp.bfloat16), preferred_element_type=jnp.float32)
    keep = ids((rows, wide), 0) % GROUP == ids((rows, wide), 1) % GROUP
    return jnp.where(keep, spread, 0.0).astype(jnp.bfloat16)


def onset_window(start, mute_ref, wide):
    parts = mute_ref.shape[0]
    flip = ids((LANES, LANES), 0) + ids((LANES, LANES), 1) == LANES - 1
    mute = mute_ref[...].astype(jnp.float32)
    back = jnp.dot(
        mute.astype(jnp.bfloat16), flip.astype(jnp.bfloat16), preferred_element_type=jnp.float32
    )
    stations = parts * LANES
    tall = 8
    behind = [jnp.broadcast_to(back[i : i + 1, :], (tall, LANES)) for i in reversed(range(parts))]
    ahead = [jnp.broadcast_to(mute[i : i + 1, :], (tall, LANES)) for i in range(parts)]
    behind = pltpu.roll(jnp.concatenate(behind, axis=1), 1, 1)
    both = jnp.concatenate([behind] + ahead, axis=1)
    return pltpu.roll(both, 2 * stations - start, 1)[:, :wide].astype(jnp.int32)


def dft_kernel(tapered, base, src_rows, rows, slots, counts, bins_ref, x_ref, mute_ref, *refs):
    outs, (window_ref, index_ref, ramp_ref, table_ref) = refs[:-4], refs[-4:]
    own_ref, outs = outs[0], outs[1:]
    samples, _, width = x_ref.shape
    wide = window_ref.shape[1]
    step = pl.program_id(0)

    @pl.when(step == 0)
    def _():
        stations = mute_ref.shape[0] * LANES
        place, side = lax.axis_index("tile"), lax.axis_index("sub")
        start = side * width - (place + 1) * src_rows + stations
        window_ref[...] = onset_window(start, mute_ref, wide)
        ramp_ref[...] = ramp_table()
        table_ref[...] = spread_table(bins_ref, place, samples, slots)

    window = jnp.broadcast_to(window_ref[0:1, :], (rows, wide))
    slanted = pltpu.roll(window, base, 1, stride=1, stride_axis=0)
    index_ref[...] = GROUP + 1 - pltpu.roll(slanted, step * rows, 1)[:, 0:width]
    ramp = ramp_ref[...]
    for s in range(0, rows, GROUP):
        columns = []
        for r in range(0, width, LANES):
            at = index_ref[s : s + GROUP, r : r + LANES]
            parts = []
            for t in range(samples):
                x = x_ref[t, s : s + GROUP, r : r + LANES]
                if t < tapered:
                    weight = jnp.take_along_axis(ramp, at + t, axis=1)
                    x = (x.astype(jnp.float32) * weight).astype(jnp.bfloat16)
                parts.append(x)
            columns.append(jnp.concatenate(parts, axis=0))
        spectra = jnp.dot(
            table_ref[...], jnp.concatenate(columns, axis=1), preferred_element_type=jnp.float32
        ).astype(jnp.bfloat16)

        def put(out_ref, d):
            for c in range(2):
                at = (d * 2 + c) * GROUP
                out_ref[c, s : s + GROUP, :] = spectra[at : at + GROUP, :]

        put(own_ref, 0)
        begin = 0
        for m, count in enumerate(counts):

            @pl.when((step >= begin) & (step < begin + count // rows))
            def _():
                for d in range(1, slots):
                    put(outs[m * (slots - 1) + d - 1], d)

            begin += count // rows


def dft(bins, traces, mute, first, counts, slots):
    samples, src_rows, width = traces.shape
    total = sum(counts)
    rows = 2 * GROUP
    while any(n % rows for n in [first] + counts):
        rows //= 2
    wide = -(-(src_rows + width) // LANES) * LANES
    tapered = min(samples, LATEST + RAMP)

    def piece(begin, count):
        last = count // rows - 1
        return pl.BlockSpec(
            (2, rows, width), lambda i, *_: (0, jnp.clip(i - begin // rows, 0, last), 0)
        )

    outs, specs = [(2, total, width)], [piece(0, total)]
    for m, count in enumerate(counts):
        outs += [(2, count, width)] * (slots - 1)
        specs += [piece(sum(counts[:m]), count)] * (slots - 1)
    return pl.pallas_call(
        functools.partial(
            dft_kernel, tapered, wide - src_rows + first, src_rows, rows, slots, counts
        ),
        grid_spec=pltpu.PrefetchScalarGridSpec(
            num_scalar_prefetch=1,
            grid=(total // rows,),
            in_specs=[
                pl.BlockSpec((samples, rows, width), lambda i, *_: (0, i + first // rows, 0)),
                pl.BlockSpec(mute.shape, lambda i, *_: (0, 0)),
            ],
            out_specs=specs,
            scratch_shapes=[
                pltpu.VMEM((8, wide), jnp.int32),
                pltpu.VMEM((rows, width), jnp.int32),
                pltpu.VMEM((GROUP, LANES), jnp.float32),
                pltpu.VMEM((slots * 2 * GROUP, samples * GROUP), jnp.bfloat16),
            ],
        ),
        out_shape=[jax.ShapeDtypeStruct(shape, jnp.bfloat16) for shape in outs],
        compiler_params=pltpu.CompilerParams(
            vmem_limit_bytes=67_043_328
        ),
        cost_estimate=pl.CostEstimate(
            flops=4 * slots * samples * total * width * GROUP,
            bytes_accessed=samples * total * width * 2,
            transcendentals=0,
        ),
    )(bins, traces, mute)


def stack_kernel(at, count, slots, packed, own_ref, *refs):
    place = lax.axis_index("tile")
    blocks, outs = (refs[:1], refs[1:]) if packed else (refs[: slots - 1], refs[slots - 1 :])
    outs[0][place] = own_ref[:, at : at + count, :]
    for d in range(1, slots):
        block = blocks[0][d - 1] if packed else blocks[d - 1][...]
        outs[0][receiver(place, d, slots)[1]] = block
        if not packed:
            outs[1][d - 1] = block


def stack(own, at, blocks, slots):
    packed = len(blocks) == 1 and slots > 2
    comps, count, cols = blocks[0].shape[-3:]
    sizes = [slots] if packed else [slots, slots - 1]
    vmem = pl.BlockSpec(memory_space=pltpu.VMEM)
    size = slots * count * comps * cols
    return pl.pallas_call(
        functools.partial(stack_kernel, at, count, slots, packed),
        in_specs=[vmem] * (1 + len(blocks)),
        out_specs=[vmem] * len(sizes),
        out_shape=[jax.ShapeDtypeStruct((n, comps, count, cols), jnp.bfloat16) for n in sizes],
        compiler_params=pltpu.CompilerParams(vmem_limit_bytes=16 * 2**20),
        cost_estimate=pl.CostEstimate(flops=size, bytes_accessed=4 * size, transcendentals=0),
    )(own, *blocks)


def square_kernel(lines, half, part, counts, *refs):
    chunks = len(counts)
    per_line = 2 * chunks
    arrays = refs[: lines * per_line]
    out_ref, sym_ref = refs[lines * per_line :]
    src_rows = sum(counts)
    stations = 2 * half
    blocks = stations // LANES
    side = lax.axis_index("sub")
    row_at = lax.axis_index("line") * part
    row_at = jnp.where(row_at // half == side, 0, half) + row_at % half
    firsts = [sum(counts[:m]) for m in range(chunks)]

    def rows_of(sources, c, a, lanes):
        inner = a * LANES % half
        tile = (side if a * LANES < half else 1 - side) * (half // src_rows) + inner // src_rows
        pieces = []
        left, row = LANES, inner % src_rows
        while left:
            take = min(left, src_rows - row)
            for first, count, source in zip(firsts, counts, sources):
                lo, hi = max(row, first), min(row + take, first + count)
                if lo < hi:
                    pieces.append(source[tile, c, lo - first : hi - first, lanes])
            left, tile, row = left - take, tile + 1, 0
        return pieces[0] if len(pieces) == 1 else jnp.concatenate(pieces, axis=0)

    for line in range(lines):
        own = range(line * per_line, (line + 1) * per_line)
        sides = [[arrays[i] for i in own[s * chunks : (s + 1) * chunks]] for s in range(2)]

        def block(c, a, b):
            at = b * LANES % half
            lanes = slice(at, at + LANES)
            return rows_of(sides[b * LANES // half], c, a, lanes).astype(jnp.float32)

        @pl.loop(0, 2)
        def _(c):
            for a in range(blocks):
                for b in range(a, blocks):
                    mean = (block(c, a, b) + block(c, b, a).T) * 0.5
                    i, j = slice(a * LANES, (a + 1) * LANES), slice(b * LANES, (b + 1) * LANES)
                    sym_ref[c, i, j] = mean.astype(jnp.bfloat16)
                    if a != b:
                        sym_ref[c, j, i] = mean.T.astype(jnp.bfloat16)

        rows = pl.ds(pl.multiple_of(row_at, part), part)
        real_left, imag_left = sym_ref[0, rows, :], sym_ref[1, rows, :]
        real_right, imag_right = sym_ref[0, :, 0:half], sym_ref[1, :, 0:half]
        dot = functools.partial(jnp.dot, preferred_element_type=jnp.float32)
        real = dot(real_left, real_right) - dot(imag_left, imag_right)
        imag = dot(real_left, imag_right) + dot(imag_left, real_right)
        factor = jnp.float32(1.0 / math.sqrt(stations))
        if line == 0:
            out_ref[0, 0], out_ref[1, 0] = real * factor, imag * factor
        else:
            out_ref[0, 0] += real * factor
            out_ref[1, 0] += imag * factor


def square(held, lines, half, counts):
    stations = 2 * half
    part = stations // lines
    return pl.pallas_call(
        functools.partial(square_kernel, lines, half, part, counts),
        in_specs=[pl.BlockSpec(memory_space=pltpu.VMEM)] * len(held),
        out_specs=pl.BlockSpec(memory_space=pltpu.VMEM),
        out_shape=jax.ShapeDtypeStruct((2, 1, part, half), jnp.float32),
        scratch_shapes=[pltpu.VMEM((2, stations, stations), jnp.bfloat16)],
        compiler_params=pltpu.CompilerParams(vmem_limit_bytes=36 * 2**20),
        cost_estimate=pl.CostEstimate(
            flops=8 * lines * part * half * stations,
            bytes_accessed=4 * lines * stations * stations,
            transcendentals=0,
        ),
    )(*held)


def shift(array, axis, step):
    count = lax.axis_size(axis)
    return lax.ppermute(array, axis, [(i, (i + step) % count) for i in range(count)])


def row_chunks(src_rows):
    units = src_rows // GROUP
    if units < 8:
        return [[src_rows]]
    last, some = units // 8, units // 4
    return [[(units - last - 2 * some) * GROUP], [some * GROUP, some * GROUP, last * GROUP]]


def send(array, distance):
    count = lax.axis_size("tile")
    pairs = [(i, receiver(i, distance, count)[0]) for i in range(count)]
    return lax.ppermute(array, "tile", pairs)


def local(traces, mute_index, freq_bins):
    src_rows, rcv_cols = traces.shape[2:]
    owners, lines = lax.axis_size("tile"), lax.axis_size("line")
    mute = mute_index.reshape(-1, LANES)
    groups = row_chunks(src_rows)
    counts = [count for group in groups for count in group]
    chunks = len(counts)
    held = [[[None] * chunks for _ in range(2)] for _ in range(lines)]
    first, made = 0, []
    for group in groups:
        own, *blocks = dft(freq_bins, traces[0], mute, first, group, owners)
        first += sum(group)
        at = 0
        passed = [shift(own, "line", e) for e in range(1, lines)]
        for m, count in enumerate(group):
            pieces = blocks[m * (owners - 1) : (m + 1) * (owners - 1)]
            arrived = [None] * (owners - 1)
            for d in reversed(range(1, owners)):
                arrived[d - 1] = send(pieces[d - 1], d)
            made.append((own, passed, at, arrived))
            at += count
    for m, (own, passed, at, arrived) in enumerate(made):
        whole, rest = stack(own, at, arrived, owners)
        held[0][0][m], held[0][1][m] = whole, shift(whole, "sub", 1)
        for e in range(1, lines):
            rest_e = shift(rest, "line", e)
            (other,) = stack(passed[e - 1], at, [rest_e], owners)
            held[e][0][m], held[e][1][m] = other, shift(other, "sub", 1)
    arrays = [array for line in held for side in line for array in side]
    return square(arrays, lines, rcv_cols, counts)


def solution(mesh):
    return jax.shard_map(
        local,
        mesh=mesh,
        in_specs=(P(("groups", "line"), None, "tile", "sub"), P(), P()),
        out_specs=P(None, "tile", ("groups", "line"), "sub"),
        check_vma=False,
    )
```

time: 121 us -> 106 us (0.88)
  the two profiles are of different devices: /device:TPU:0 before, /device:TPU:19 now
where the time goes in v2:
time: 106 us
  waiting for transfers between devices  40 us (38%)
  Pallas kernels  33.1 us (31%)
  starting transfers between devices  30 us (28%)
  local copies, waits for them, and re-layouts  2.87 us (3%)
    pallas_call x2, Pallas kernels, dft(): pl.pallas_call(functools.partial(dft_kernel, tapered, wide - src_rows + f...  22.6 us
    ppermute x14, waiting for transfers between devices, shift(): lax.ppermute(array, axis, [(i, (i + step) % count) for i in range(count)])  21.4 us
    ppermute x14, starting transfers between devices, shift(): lax.ppermute(array, axis, [(i, (i + step) % count) for i in range(count)])  20.2 us
    ppermute x12, waiting for transfers between devices, send(): return lax.ppermute(array, 'tile', pairs)  18.6 us
    ppermute x12, starting transfers between devices, send(): return lax.ppermute(array, 'tile', pairs)  9.8 us
    pallas_call x1, Pallas kernels, square(): pl.pallas_call(functools.partial(square_kernel, lines, half, part, counts...  8.93 us
    unnamed x6, local copies, waits for them, and re-layouts  2.87 us
  transfers between devices with their start and end apart: 26, of which 11 were waited for; matrix products, arithmetic and copies ran while one was open for 0% of the time, Pallas kernels for 14%

profile of v2, /device:TPU:19, one launch (start us, length us, event | category | flops | bytes accessed | tf_op | source)
XLA Modules:
  0.0 105.9 jit_solution(210524003215081265)
XLA Ops:
  0.0 9.1 %shard_map.37 = (bf16[2,96,512]{2,1,0:T(8,128)(2,1)}, bf16[2,96,512]{2,1,0:T(8,128)(2,1)}, bf16[2,96,512]{2,1,0:T(8,128)(2,1)}, bf16[2,96,512]{2,1,0:T(8,128)(2,1)}) custom-call(s32[4]{0:T(128)} %bins_ref.3, bf16[64,256,512]{2,1,0:T(8,128)(2,1)} %bitcast.2, s32[8,128]{1,0:T(8,128)} %bitcast.4), custom_call_target="tpu_custom_call" | custom-call | flops 805306368 | bytes 6291456 | tf_op jit(solution)/shard_map/pallas_call | solution.py:140
  9.1 1.3 %collective-permute-start = (bf16[2,96,512]{2,1,0:T(8,128)(2,1)}, bf16[2,96,512]{2,1,0:T(8,128)(2,1)}, u32[]{:S(2)}, u32[]{:S(2)}) collective-permute-start(bf16[2,96,512]{2,1,0:T(8,128)(2,1)} %get-tuple-element.28), channel_id=1, source_target_pairs={{0,4},{4,0},{8,12},{12,8},{1,5},{5,1},{9,13},{13,9},{2,6},{6,2},{1... | collective-permute-start | bytes 589832 | tf_op jit(solution)/shard_map/ppermute | solution.py:292
  10.4 0.1 collective-permute-start.1
  10.5 1.3 %collective-permute-start.2 = (bf16[2,96,512]{2,1,0:T(8,128)(2,1)}, bf16[2,96,512]{2,1,0:T(8,128)(2,1)}, u32[]{:S(2)}, u32[]{:S(2)}) collective-permute-start(bf16[2,96,512]{2,1,0:T(8,128)(2,1)} %get-tuple-element.30), channel_id=1, source_target_pairs={{0,12},{4,8},{8,4},{12,0},{1,13},{5,9},{9,5},{13,1},{2,14},{6,10},... | collective-permute-start | bytes 589832 | tf_op jit(solution)/shard_map/ppermute | solution.py:292
  11.8 13.5 %shard_map.39 = (bf16[2,160,512]{2,1,0:T(8,128)(2,1)}, bf16[2,64,512]{2,1,0:T(8,128)(2,1)}, bf16[2,64,512]{2,1,0:T(8,128)(2,1)}, bf16[2,64,512]{2,1,0:T(8,128)(2...) custom-call(s32[4]{0:T(128)} %bins_ref.3, ...), custom_call_target="tpu_custom_call" | custom-call | flops 1342177280 | bytes 10485760 | tf_op jit(solution)/shard_map/pallas_call | solution.py:140
  25.2 2.2 %collective-permute-start.9 = (bf16[2,32,512]{2,1,0:T(8,128)(2,1)}, bf16[2,32,512]{2,1,0:T(8,128)(2,1)S(1)}, u32[]{:S(2)}, u32[]{:S(2)}) collective-permute-start(bf16[2,32,512]{2,1,0:T(8,128)(2,1)} %get-tuple-element.41), channel_id=1, source_target_pairs={{0,4},{4,0},{8,12},{12,8},{1,5},{5,1},{9,13},{13,9},{2,6},{6,2},{1... | collective-permute-start | bytes 196616 | tf_op jit(solution)/shard_map/ppermute | solution.py:292
  27.5 0.0 collective-permute-start.10
  27.5 2.3 %collective-permute-done.9.refs_0_ = bf16[2,32,512]{2,1,0:T(8,128)(2,1)S(1)} collective-permute-done((bf16[2,32,512]{2,1,0:T(8,128)(2,1)}, bf16[2,32,512]{2,1,0:T(8,128)(2,1)S(1)}, u32[]{:S(2)}, u32[]{:S(2)}) %collective-permute-start.9) | collective-permute-done | bytes 65568 | tf_op jit(solution)/shard_map/ppermute | solution.py:292
  29.8 1.1 %collective-permute-start.3 = (bf16[2,64,512]{2,1,0:T(8,128)(2,1)}, bf16[2,64,512]{2,1,0:T(8,128)(2,1)S(1)}, u32[]{:S(2)}, u32[]{:S(2)}) collective-permute-start(bf16[2,64,512]{2,1,0:T(8,128)(2,1)} %get-tuple-element.33), channel_id=1, source_target_pairs={{0,4},{4,0},{8,12},{12,8},{1,5},{5,1},{9,13},{13,9},{2,6},{6,2},{1... | collective-permute-start | bytes 393224 | tf_op jit(solution)/shard_map/ppermute | solution.py:292
  30.8 0.0 collective-permute-done.refs_0_
  30.8 0.0 collective-permute-start.4
  30.8 0.0 collective-permute-done.1.refs_1_
  30.8 1.6 %collective-permute-start.11 = (bf16[2,32,512]{2,1,0:T(8,128)(2,1)}, bf16[2,32,512]{2,1,0:T(8,128)(2,1)S(1)}, u32[]{:S(2)}, u32[]{:S(2)}) collective-permute-start(bf16[2,32,512]{2,1,0:T(8,128)(2,1)} %get-tuple-element.43), channel_id=1, source_target_pairs={{0,12},{4,8},{8,4},{12,0},{1,13},{5,9},{9,5},{13,1},{2,14},{6,10},... | collective-permute-start | bytes 196616 | tf_op jit(solution)/shard_map/ppermute | solution.py:292
  32.4 0.1 collective-permute-start.5
  32.5 0.9 copy-done.2
  33.4 1.2 %shard_map.38 = (bf16[4,2,96,512]{3,2,1,0:T(8,128)(2,1)S(1)}, bf16[3,2,96,512]{3,2,1,0:T(8,128)(2,1)S(1)}) custom-call(bf16[2,96,512]{2,1,0:T(8,128)(2,1)S(1)} %copy-done.2, bf16[2,96,512]{2,1,0:T(8,128)(2,1)} %collective-permute-done.refs_0_, bf16[2,96,512]{2,1,0:T(8,128)(2,1)} %collective-permute-done.1.refs_1_, ...), custom_call_target="tpu_custom_call" | custom-call | flops 393216 | bytes 1572864 | tf_op jit(solution)/shard_map/pallas_call | solution.py:188
  34.6 2.2 %collective-permute-start.6 = (bf16[2,64,512]{2,1,0:T(8,128)(2,1)}, bf16[2,64,512]{2,1,0:T(8,128)(2,1)S(1)}, u32[]{:S(2)}, u32[]{:S(2)}) collective-permute-start(bf16[2,64,512]{2,1,0:T(8,128)(2,1)} %get-tuple-element.37), channel_id=1, source_target_pairs={{0,4},{4,0},{8,12},{12,8},{1,5},{5,1},{9,13},{13,9},{2,6},{6,2},{1... | collective-permute-start | bytes 393224 | tf_op jit(solution)/shard_map/ppermute | solution.py:292
  36.8 6.1 %collective-permute-done.11.refs_2_ = bf16[2,32,512]{2,1,0:T(8,128)(2,1)S(1)} collective-permute-done((bf16[2,32,512]{2,1,0:T(8,128)(2,1)}, bf16[2,32,512]{2,1,0:T(8,128)(2,1)S(1)}, u32[]{:S(2)}, u32[]{:S(2)}) %collective-permute-start.11) | collective-permute-done | bytes 65568 | tf_op jit(solution)/shard_map/ppermute | solution.py:292
  42.9 0.3 collective-permute-start.17
  43.2 1.2 %collective-permute-start.18 = (bf16[2,160,512]{2,1,0:T(8,128)(2,1)}, bf16[2,160,512]{2,1,0:T(8,128)(2,1)S(1)}, u32[]{:S(2)}, u32[]{:S(2)}) collective-permute-start(bf16[2,160,512]{2,1,0:T(8,128)(2,1)} %get-tuple-element.32.own_ref), channel_id=1, source_target_pairs={{0,2},{2,0},{1,3},{3,1},{4,6},{6,4},{5,7},{7,5},{8,10},{10,8},{9,1... | collective-permute-start | bytes 983048 | tf_op jit(solution)/shard_map/ppermute | solution.py:278
  44.4 2.5 %collective-permute-done.5.refs_2_ = bf16[2,64,512]{2,1,0:T(8,128)(2,1)S(1)} collective-permute-done((bf16[2,64,512]{2,1,0:T(8,128)(2,1)}, bf16[2,64,512]{2,1,0:T(8,128)(2,1)S(1)}, u32[]{:S(2)}, u32[]{:S(2)}) %collective-permute-start.5) | collective-permute-done | bytes 131104 | tf_op jit(solution)/shard_map/ppermute | solution.py:292
  47.0 1.0 copy-done
  48.0 0.3 collective-permute-start.21
  48.3 1.0 copy-done.1
  49.3 0.1 shard_map.40
  49.3 0.1 collective-permute-done.7.refs_1_
  49.4 1.2 %collective-permute-start.19 = (bf16[3,2,64,512]{3,2,1,0:T(8,128)(2,1)S(1)}, bf16[3,2,64,512]{3,2,1,0:T(8,128)(2,1)S(1)}, u32[]{:S(2)}, u32[]{:S(2)}) collective-permute-start(bf16[3,2,64,512]{3,2,1,0:T(8,128)(2,1)S(1)} %get-tuple-element.46), channel_id=1, source_target_pairs={{0,2},{2,0},{1,3},{3,1},{4,6},{6,4},{5,7},{7,5},{8,10},{10,8},{9,1... | collective-permute-start | bytes 1179656 | tf_op jit(solution)/shard_map/ppermute | solution.py:278
  50.6 7.6 %collective-permute-done.8.refs_2_ = bf16[2,64,512]{2,1,0:T(8,128)(2,1)S(1)} collective-permute-done((bf16[2,64,512]{2,1,0:T(8,128)(2,1)}, bf16[2,64,512]{2,1,0:T(8,128)(2,1)S(1)}, u32[]{:S(2)}, u32[]{:S(2)}) %collective-permute-start.8) | collective-permute-done | bytes 131104 | tf_op jit(solution)/shard_map/ppermute | solution.py:292
  58.2 0.1 shard_map.41
  58.3 0.3 collective-permute-start.20
  58.6 6.2 %collective-permute-done.21.refs_0_ = bf16[3,2,32,512]{3,2,1,0:T(8,128)(2,1)S(1)} collective-permute-done((bf16[3,2,32,512]{3,2,1,0:T(8,128)(2,1)S(1)}, bf16[3,2,32,512]{3,2,1,0:T(8,128)(2,1)S(1)}, u32[]{:S(2)}, u32[]{:S(2)}) %collective-permute-start.21) | collective-permute-done | bytes 196640 | tf_op jit(solution)/shard_map/ppermute | solution.py:278
  64.8 9.9 %collective-permute-start.13 = (bf16[4,2,64,512]{3,2,1,0:T(8,128)(2,1)S(1)}, bf16[4,2,64,512]{3,2,1,0:T(8,128)(2,1)S(1)}, u32[]{:S(2)}, u32[]{:S(2)}) collective-permute-start(bf16[4,2,64,512]{3,2,1,0:T(8,128)(2,1)S(1)} %get-tuple-element.36.refs_1_), channel_id=1, source_target_pairs={{0,1},{1,0},{2,3},{3,2},{4,5},{5,4},{6,7},{7,6},{8,9},{9,8},{10,11... | collective-permute-start | bytes 1572872 | tf_op jit(solution)/shard_map/ppermute | solution.py:278
  74.7 0.3 collective-permute-start.16
  75.0 10.9 %collective-permute-done.16.own_ref = bf16[2,96,512]{2,1,0:T(8,128)(2,1)S(1)} collective-permute-done((bf16[2,96,512]{2,1,0:T(8,128)(2,1)}, bf16[2,96,512]{2,1,0:T(8,128)(2,1)S(1)}, u32[]{:S(2)}, u32[]{:S(2)}) %collective-permute-start.16) | collective-permute-done | bytes 196640 | tf_op jit(solution)/shard_map/ppermute | solution.py:278
  85.8 5.2 %collective-permute-start.15 = (bf16[4,2,32,512]{3,2,1,0:T(8,128)(2,1)S(1)}, bf16[4,2,32,512]{3,2,1,0:T(8,128)(2,1)S(1)}, u32[]{:S(2)}, u32[]{:S(2)}) collective-permute-start(bf16[4,2,32,512]{3,2,1,0:T(8,128)(2,1)S(1)} %get-tuple-element.44.refs_3_), channel_id=1, source_target_pairs={{0,1},{1,0},{2,3},{3,2},{4,5},{5,4},{6,7},{7,6},{8,9},{9,8},{10,11... | collective-permute-start | bytes 786440 | tf_op jit(solution)/shard_map/ppermute | solution.py:278
  91.0 0.0 collective-permute-start.25
  91.0 0.5 collective-permute-start.12
  91.5 0.1 shard_map.43.refs_8_
  91.6 0.1 collective-permute-start.22
  91.8 0.3 collective-permute-done.15.refs_7_
  92.1 0.4 collective-permute-start.14
  92.5 0.0 collective-permute-done.25.refs_15_
  92.5 0.4 collective-permute-start.24
  92.9 0.1 collective-permute-start.23
  93.0 2.5 %collective-permute-done.14.refs_6_ = bf16[4,2,64,512]{3,2,1,0:T(8,128)(2,1)S(1)} collective-permute-done((bf16[4,2,64,512]{3,2,1,0:T(8,128)(2,1)S(1)}, bf16[4,2,64,512]{3,2,1,0:T(8,128)(2,1)S(1)}, u32[]{:S(2)}, u32[]{:S(2)}) %collective-permute-start.14) | collective-permute-done | bytes 524320 | tf_op jit(solution)/shard_map/ppermute | solution.py:278
  95.5 0.7 collective-permute-done.24.refs_14_
  96.3 0.7 collective-permute-done.23.refs_13_
  97.0 8.9 %shard_map.47 = f32[2,1,512,512]{3,2,1,0:T(8,128)} custom-call(bf16[4,2,96,512]{3,2,1,0:T(8,128)(2,1)S(1)} %get-tuple-element.31.refs_0_, bf16[4,2,64,512]{3,2,1,0:T(8,128)(2,1)S(1)} %get-tuple-element.36.refs_1_, bf16[4,2,64,512]{3,2,1,0:T(8,128)(2,1)S(1)} %get-tuple-element.40.refs_2_, bf16[4,2,32,512]{3,2,1,0:T(8,128)(2,1)S(1)} %get-tuple-element.44.refs_3_, ...), custom_call_target="tpu_custom_call" | custom-call | flops 4294967296 | bytes 8388608 | tf_op jit(solution)/shard_map/pallas_call | solution.py:261
  (21 shorter events, 0.2 us)
Async XLA Ops:
  9.1 21.7 %collective-permute-start = (bf16[2,96,512]{2,1,0:T(8,128)(2,1)}, bf16[2,96,512]{2,1,0:T(8,128)(2,1)}, u32[]{:S(2)}, u32[]{:S(2)}) collective-permute-start(bf16[2,96,512]{2,1,0:T(8,128)(2,1)} %get-tuple-element.28), channel_id=1, source_target_pairs={{0,4},{4,0},{8,12},{12,8},{1,5},{5,1},{9,13},{13,9},{2,6},{6,2},{1... | collective-permute-start | bytes 589832 | tf_op jit(solution)/shard_map/ppermute | solution.py:292
  10.4 20.4 %collective-permute-start.1 = (bf16[2,96,512]{2,1,0:T(8,128)(2,1)}, bf16[2,96,512]{2,1,0:T(8,128)(2,1)}, u32[]{:S(2)}, u32[]{:S(2)}) collective-permute-start(bf16[2,96,512]{2,1,0:T(8,128)(2,1)} %get-tuple-element.29), channel_id=1, source_target_pairs={{0,8},{4,12},{8,0},{12,4},{1,9},{5,13},{9,1},{13,5},{2,10},{6,14},... | collective-permute-start | bytes 589832 | tf_op jit(solution)/shard_map/ppermute | solution.py:292
  10.5 21.9 %collective-permute-start.2 = (bf16[2,96,512]{2,1,0:T(8,128)(2,1)}, bf16[2,96,512]{2,1,0:T(8,128)(2,1)}, u32[]{:S(2)}, u32[]{:S(2)}) collective-permute-start(bf16[2,96,512]{2,1,0:T(8,128)(2,1)} %get-tuple-element.30), channel_id=1, source_target_pairs={{0,12},{4,8},{8,4},{12,0},{1,13},{5,9},{9,5},{13,1},{2,14},{6,10},... | collective-permute-start | bytes 589832 | tf_op jit(solution)/shard_map/ppermute | solution.py:292
  25.2 4.5 %collective-permute-start.9 = (bf16[2,32,512]{2,1,0:T(8,128)(2,1)}, bf16[2,32,512]{2,1,0:T(8,128)(2,1)S(1)}, u32[]{:S(2)}, u32[]{:S(2)}) collective-permute-start(bf16[2,32,512]{2,1,0:T(8,128)(2,1)} %get-tuple-element.41), channel_id=1, source_target_pairs={{0,4},{4,0},{8,12},{12,8},{1,5},{5,1},{9,13},{13,9},{2,6},{6,2},{1... | collective-permute-start | bytes 196616 | tf_op jit(solution)/shard_map/ppermute | solution.py:292
  27.5 7.1 %collective-permute-start.10 = (bf16[2,32,512]{2,1,0:T(8,128)(2,1)}, bf16[2,32,512]{2,1,0:T(8,128)(2,1)S(1)}, u32[]{:S(2)}, u32[]{:S(2)}) collective-permute-start(bf16[2,32,512]{2,1,0:T(8,128)(2,1)} %get-tuple-element.42), channel_id=1, source_target_pairs={{0,8},{4,12},{8,0},{12,4},{1,9},{5,13},{9,1},{13,5},{2,10},{6,14},... | collective-permute-start | bytes 196616 | tf_op jit(solution)/shard_map/ppermute | solution.py:292
  29.8 13.4 %collective-permute-start.3 = (bf16[2,64,512]{2,1,0:T(8,128)(2,1)}, bf16[2,64,512]{2,1,0:T(8,128)(2,1)S(1)}, u32[]{:S(2)}, u32[]{:S(2)}) collective-permute-start(bf16[2,64,512]{2,1,0:T(8,128)(2,1)} %get-tuple-element.33), channel_id=1, source_target_pairs={{0,4},{4,0},{8,12},{12,8},{1,5},{5,1},{9,13},{13,9},{2,6},{6,2},{1... | collective-permute-start | bytes 393224 | tf_op jit(solution)/shard_map/ppermute | solution.py:292
  30.8 13.6 %collective-permute-start.4 = (bf16[2,64,512]{2,1,0:T(8,128)(2,1)}, bf16[2,64,512]{2,1,0:T(8,128)(2,1)S(1)}, u32[]{:S(2)}, u32[]{:S(2)}) collective-permute-start(bf16[2,64,512]{2,1,0:T(8,128)(2,1)} %get-tuple-element.34), channel_id=1, source_target_pairs={{0,8},{4,12},{8,0},{12,4},{1,9},{5,13},{9,1},{13,5},{2,10},{6,14},... | collective-permute-start | bytes 393224 | tf_op jit(solution)/shard_map/ppermute | solution.py:292
  30.8 12.1 %collective-permute-start.11 = (bf16[2,32,512]{2,1,0:T(8,128)(2,1)}, bf16[2,32,512]{2,1,0:T(8,128)(2,1)S(1)}, u32[]{:S(2)}, u32[]{:S(2)}) collective-permute-start(bf16[2,32,512]{2,1,0:T(8,128)(2,1)} %get-tuple-element.43), channel_id=1, source_target_pairs={{0,12},{4,8},{8,4},{12,0},{1,13},{5,9},{9,5},{13,1},{2,14},{6,10},... | collective-permute-start | bytes 196616 | tf_op jit(solution)/shard_map/ppermute | solution.py:292
  32.4 14.5 %collective-permute-start.5 = (bf16[2,64,512]{2,1,0:T(8,128)(2,1)}, bf16[2,64,512]{2,1,0:T(8,128)(2,1)S(1)}, u32[]{:S(2)}, u32[]{:S(2)}) collective-permute-start(bf16[2,64,512]{2,1,0:T(8,128)(2,1)} %get-tuple-element.35), channel_id=1, source_target_pairs={{0,12},{4,8},{8,4},{12,0},{1,13},{5,9},{9,5},{13,1},{2,14},{6,10},... | collective-permute-start | bytes 393224 | tf_op jit(solution)/shard_map/ppermute | solution.py:292
  32.5 0.9 copy-start.2
  34.6 13.3 %collective-permute-start.6 = (bf16[2,64,512]{2,1,0:T(8,128)(2,1)}, bf16[2,64,512]{2,1,0:T(8,128)(2,1)S(1)}, u32[]{:S(2)}, u32[]{:S(2)}) collective-permute-start(bf16[2,64,512]{2,1,0:T(8,128)(2,1)} %get-tuple-element.37), channel_id=1, source_target_pairs={{0,4},{4,0},{8,12},{12,8},{1,5},{5,1},{9,13},{13,9},{2,6},{6,2},{1... | collective-permute-start | bytes 393224 | tf_op jit(solution)/shard_map/ppermute | solution.py:292
  42.9 48.1 %collective-permute-start.17 = (bf16[3,2,96,512]{3,2,1,0:T(8,128)(2,1)S(1)}, bf16[3,2,96,512]{3,2,1,0:T(8,128)(2,1)S(1)}, u32[]{:S(2)}, u32[]{:S(2)}) collective-permute-start(bf16[3,2,96,512]{3,2,1,0:T(8,128)(2,1)S(1)} %get-tuple-element.45), channel_id=1, source_target_pairs={{0,2},{2,0},{1,3},{3,1},{4,6},{6,4},{5,7},{7,5},{8,10},{10,8},{9,1... | collective-permute-start | bytes 1769480 | tf_op jit(solution)/shard_map/ppermute | solution.py:278
  43.2 31.5 %collective-permute-start.18 = (bf16[2,160,512]{2,1,0:T(8,128)(2,1)}, bf16[2,160,512]{2,1,0:T(8,128)(2,1)S(1)}, u32[]{:S(2)}, u32[]{:S(2)}) collective-permute-start(bf16[2,160,512]{2,1,0:T(8,128)(2,1)} %get-tuple-element.32.own_ref), channel_id=1, source_target_pairs={{0,2},{2,0},{1,3},{3,1},{4,6},{6,4},{5,7},{7,5},{8,10},{10,8},{9,1... | collective-permute-start | bytes 983048 | tf_op jit(solution)/shard_map/ppermute | solution.py:278
  44.4 5.0 %collective-permute-start.7 = (bf16[2,64,512]{2,1,0:T(8,128)(2,1)}, bf16[2,64,512]{2,1,0:T(8,128)(2,1)S(1)}, u32[]{:S(2)}, u32[]{:S(2)}) collective-permute-start(bf16[2,64,512]{2,1,0:T(8,128)(2,1)} %get-tuple-element.38), channel_id=1, source_target_pairs={{0,8},{4,12},{8,0},{12,4},{1,9},{5,13},{9,1},{13,5},{2,10},{6,14},... | collective-permute-start | bytes 393224 | tf_op jit(solution)/shard_map/ppermute | solution.py:292
  47.0 11.2 %collective-permute-start.8 = (bf16[2,64,512]{2,1,0:T(8,128)(2,1)}, bf16[2,64,512]{2,1,0:T(8,128)(2,1)S(1)}, u32[]{:S(2)}, u32[]{:S(2)}) collective-permute-start(bf16[2,64,512]{2,1,0:T(8,128)(2,1)} %get-tuple-element.39), channel_id=1, source_target_pairs={{0,12},{4,8},{8,4},{12,0},{1,13},{5,9},{9,5},{13,1},{2,14},{6,10},... | collective-permute-start | bytes 393224 | tf_op jit(solution)/shard_map/ppermute | solution.py:292
  47.0 1.0 copy-start
  48.0 16.8 %collective-permute-start.21 = (bf16[3,2,32,512]{3,2,1,0:T(8,128)(2,1)S(1)}, bf16[3,2,32,512]{3,2,1,0:T(8,128)(2,1)S(1)}, u32[]{:S(2)}, u32[]{:S(2)}) collective-permute-start(bf16[3,2,32,512]{3,2,1,0:T(8,128)(2,1)S(1)} %get-tuple-element.48), channel_id=1, source_target_pairs={{0,2},{2,0},{1,3},{3,1},{4,6},{6,4},{5,7},{7,5},{8,10},{10,8},{9,1... | collective-permute-start | bytes 589832 | tf_op jit(solution)/shard_map/ppermute | solution.py:278
  48.3 1.0 copy-start.1
  49.4 41.5 %collective-permute-start.19 = (bf16[3,2,64,512]{3,2,1,0:T(8,128)(2,1)S(1)}, bf16[3,2,64,512]{3,2,1,0:T(8,128)(2,1)S(1)}, u32[]{:S(2)}, u32[]{:S(2)}) collective-permute-start(bf16[3,2,64,512]{3,2,1,0:T(8,128)(2,1)S(1)} %get-tuple-element.46), channel_id=1, source_target_pairs={{0,2},{2,0},{1,3},{3,1},{4,6},{6,4},{5,7},{7,5},{8,10},{10,8},{9,1... | collective-permute-start | bytes 1179656 | tf_op jit(solution)/shard_map/ppermute | solution.py:278
  58.3 33.3 %collective-permute-start.20 = (bf16[3,2,64,512]{3,2,1,0:T(8,128)(2,1)S(1)}, bf16[3,2,64,512]{3,2,1,0:T(8,128)(2,1)S(1)}, u32[]{:S(2)}, u32[]{:S(2)}) collective-permute-start(bf16[3,2,64,512]{3,2,1,0:T(8,128)(2,1)S(1)} %get-tuple-element.47), channel_id=1, source_target_pairs={{0,2},{2,0},{1,3},{3,1},{4,6},{6,4},{5,7},{7,5},{8,10},{10,8},{9,1... | collective-permute-start | bytes 1179656 | tf_op jit(solution)/shard_map/ppermute | solution.py:278
  64.8 28.1 %collective-permute-start.13 = (bf16[4,2,64,512]{3,2,1,0:T(8,128)(2,1)S(1)}, bf16[4,2,64,512]{3,2,1,0:T(8,128)(2,1)S(1)}, u32[]{:S(2)}, u32[]{:S(2)}) collective-permute-start(bf16[4,2,64,512]{3,2,1,0:T(8,128)(2,1)S(1)} %get-tuple-element.36.refs_1_), channel_id=1, source_target_pairs={{0,1},{1,0},{2,3},{3,2},{4,5},{5,4},{6,7},{7,6},{8,9},{9,8},{10,11... | collective-permute-start | bytes 1572872 | tf_op jit(solution)/shard_map/ppermute | solution.py:278
  74.7 11.1 %collective-permute-start.16 = (bf16[2,96,512]{2,1,0:T(8,128)(2,1)}, bf16[2,96,512]{2,1,0:T(8,128)(2,1)S(1)}, u32[]{:S(2)}, u32[]{:S(2)}) collective-permute-start(bf16[2,96,512]{2,1,0:T(8,128)(2,1)} %get-tuple-element.27.own_ref), channel_id=1, source_target_pairs={{0,2},{2,0},{1,3},{3,1},{4,6},{6,4},{5,7},{7,5},{8,10},{10,8},{9,1... | collective-permute-start | bytes 589832 | tf_op jit(solution)/shard_map/ppermute | solution.py:278
  85.8 6.3 %collective-permute-start.15 = (bf16[4,2,32,512]{3,2,1,0:T(8,128)(2,1)S(1)}, bf16[4,2,32,512]{3,2,1,0:T(8,128)(2,1)S(1)}, u32[]{:S(2)}, u32[]{:S(2)}) collective-permute-start(bf16[4,2,32,512]{3,2,1,0:T(8,128)(2,1)S(1)} %get-tuple-element.44.refs_3_), channel_id=1, source_target_pairs={{0,1},{1,0},{2,3},{3,2},{4,5},{5,4},{6,7},{7,6},{8,9},{9,8},{10,11... | collective-permute-start | bytes 786440 | tf_op jit(solution)/shard_map/ppermute | solution.py:278
  91.0 1.5 %collective-permute-start.25 = (bf16[4,2,32,512]{3,2,1,0:T(8,128)(2,1)S(1)}, bf16[4,2,32,512]{3,2,1,0:T(8,128)(2,1)S(1)}, u32[]{:S(2)}, u32[]{:S(2)}) collective-permute-start(bf16[4,2,32,512]{3,2,1,0:T(8,128)(2,1)S(1)} %shard_map.46.refs_11_), channel_id=1, source_target_pairs={{0,1},{1,0},{2,3},{3,2},{4,5},{5,4},{6,7},{7,6},{8,9},{9,8},{10,11... | collective-permute-start | bytes 786440 | tf_op jit(solution)/shard_map/ppermute | solution.py:278
  91.0 4.5 %collective-permute-start.12 = (bf16[4,2,96,512]{3,2,1,0:T(8,128)(2,1)S(1)}, bf16[4,2,96,512]{3,2,1,0:T(8,128)(2,1)S(1)}, u32[]{:S(2)}, u32[]{:S(2)}) collective-permute-start(bf16[4,2,96,512]{3,2,1,0:T(8,128)(2,1)S(1)} %get-tuple-element.31.refs_0_), channel_id=1, source_target_pairs={{0,1},{1,0},{2,3},{3,2},{4,5},{5,4},{6,7},{7,6},{8,9},{9,8},{10,11... | collective-permute-start | bytes 2359304 | tf_op jit(solution)/shard_map/ppermute | solution.py:278
  91.6 5.4 %collective-permute-start.22 = (bf16[4,2,96,512]{3,2,1,0:T(8,128)(2,1)S(1)}, bf16[4,2,96,512]{3,2,1,0:T(8,128)(2,1)S(1)}, u32[]{:S(2)}, u32[]{:S(2)}) collective-permute-start(bf16[4,2,96,512]{3,2,1,0:T(8,128)(2,1)S(1)} %shard_map.43.refs_8_), channel_id=1, source_target_pairs={{0,1},{1,0},{2,3},{3,2},{4,5},{5,4},{6,7},{7,6},{8,9},{9,8},{10,11... | collective-permute-start | bytes 2359304 | tf_op jit(solution)/shard_map/ppermute | solution.py:278
  92.1 3.4 %collective-permute-start.14 = (bf16[4,2,64,512]{3,2,1,0:T(8,128)(2,1)S(1)}, bf16[4,2,64,512]{3,2,1,0:T(8,128)(2,1)S(1)}, u32[]{:S(2)}, u32[]{:S(2)}) collective-permute-start(bf16[4,2,64,512]{3,2,1,0:T(8,128)(2,1)S(1)} %get-tuple-element.40.refs_2_), channel_id=1, source_target_pairs={{0,1},{1,0},{2,3},{3,2},{4,5},{5,4},{6,7},{7,6},{8,9},{9,8},{10,11... | collective-permute-start | bytes 1572872 | tf_op jit(solution)/shard_map/ppermute | solution.py:278
  92.5 3.7 %collective-permute-start.24 = (bf16[4,2,64,512]{3,2,1,0:T(8,128)(2,1)S(1)}, bf16[4,2,64,512]{3,2,1,0:T(8,128)(2,1)S(1)}, u32[]{:S(2)}, u32[]{:S(2)}) collective-permute-start(bf16[4,2,64,512]{3,2,1,0:T(8,128)(2,1)S(1)} %shard_map.45.refs_10_), channel_id=1, source_target_pairs={{0,1},{1,0},{2,3},{3,2},{4,5},{5,4},{6,7},{7,6},{8,9},{9,8},{10,11... | collective-permute-start | bytes 1572872 | tf_op jit(solution)/shard_map/ppermute | solution.py:278
  92.9 4.1 %collective-permute-start.23 = (bf16[4,2,64,512]{3,2,1,0:T(8,128)(2,1)S(1)}, bf16[4,2,64,512]{3,2,1,0:T(8,128)(2,1)S(1)}, u32[]{:S(2)}, u32[]{:S(2)}) collective-permute-start(bf16[4,2,64,512]{3,2,1,0:T(8,128)(2,1)S(1)} %shard_map.44.refs_9_), channel_id=1, source_target_pairs={{0,1},{1,0},{2,3},{3,2},{4,5},{5,4},{6,7},{7,6},{8,9},{9,8},{10,11... | collective-permute-start | bytes 1572872 | tf_op jit(solution)/shard_map/ppermute | solution.py:278
